TPU v7x, 128 devices: a whole 4x4x4 slice. The times are simulated.
128 devices in a mesh: section: 2 (over x_hi), tp: 2 (over core), dp: 32 (over z, y, x_lo).
Axes of the slice: x: 4 (x_hi: 2, x_lo: 2; x = x_hi * 2 + x_lo), y: 4, z: 4, core: 2. Of those that a mesh axis runs over, the one named last changes fastest.
Arguments:
- tokens_in: bfloat16 [32, 512, 4096], P('dp', None, 'tp'), may hold values from -6 to 6
- patches: bfloat16 [32, 256, 32], P('dp'), may hold values from -6 to 6
- segment_ids: int32 [32, 512], P('dp'), may hold values from 0 to 3, never falling along the last dimension, each value on 1 to 256 neighbouring positions
- img_start: int32 [32], P('dp'), may hold values from 0 to 256
- img_count: int32 [32], P('dp'), may hold values from 0 to 1
- norm_gain: float32 [2, 4096], P('section'), may hold values from 0.1 to 1.9
- w_qkv: bfloat16 [2, 4096, 16, 3, 128], P('section', 'dp', 'tp'), may hold values from -2 to 2
- w_out: bfloat16 [2, 2048, 4096], P('section', 'dp', 'tp'), may hold values from -0.125 to 0.125
- w_down1: bfloat16 [32, 512], replicated, may hold values from -1 to 1
- w_down2: bfloat16 [512, 4096], P(None, 'tp'), may hold values from -0.25 to 0.25
- w_up1: bfloat16 [4096, 512], P('tp'), may hold values from -0.09375 to 0.09375
- w_up2: bfloat16 [512, 32], P(None, 'section'), may hold values from -0.25 to 0.25
- cotangent: bfloat16 [32, 256, 32], P('dp', None, 'section'), may hold values from -6 to 6
Outputs:
- hidden_states: bfloat16 [2, 32, 512, 4096], P('section', 'dp', None, 'tp')
- image_pred: bfloat16 [32, 256, 32], P('dp', None, 'section')
- grad_up: float32 [512, 32], P(None, 'section')
Inputs may be any that keep to these rules, and one draw needn't show every extreme that they name: `segment_ids`: document of each position; never falls along a micro-batch, each document covers 1 to 256 positions.
All inputs are finite; a program needn't handle non-finite values.
Results may differ from a plain program's by a relative error of at most 0.019.
Values may be sent and summed in bfloat16 or wider, within the bound.
A program may use at most 128 MiB of HBM per device.

v0:
```python
import math

import jax
import jax.numpy as jnp
from jax import lax
from jax.sharding import PartitionSpec as P

EPSILON = 1e-05


def passed_along(value, axis, by):
    count = lax.axis_size(axis)
    pairs = [(i, i + by) for i in range(count) if 0 <= i + by < count]
    return lax.ppermute(value, axis, pairs)


def broadcast(block, axis, holder):
    block = jnp.where(lax.axis_index(axis) == holder, block, jnp.zeros_like(block))
    return lax.psum(block, axis)


def unet_down(patches, w_down1, w_down2):
    inner = jnp.einsum("mkp,pc->mkc", patches, w_down1, preferred_element_type=jnp.float32)
    skipped = jax.nn.silu(inner).astype(jnp.bfloat16)
    tokens = jnp.einsum("mkc,cd->mkd", skipped, w_down2, preferred_element_type=jnp.float32)
    return (skipped, tokens.astype(jnp.bfloat16))


def place_images(tokens_in, image_tokens, img_start, img_count):

    def single(rows, image, start, count):
        placed = lax.dynamic_update_slice_in_dim(rows, image, start, 0)
        return jnp.where(count > 0, placed, rows)

    return jax.vmap(single)(tokens_in, image_tokens, img_start, img_count)


def allowed_pairs(segment, start, count, rows, img_tok):
    position = jnp.arange(rows, dtype=jnp.int32)
    in_image = (count > 0) & (position >= start) & (position < start + img_tok)
    same = segment[:, None] == segment[None, :]
    causal = position[None, :] <= position[:, None]
    return same & (causal | in_image[:, None] & in_image[None, :])


def rms_normed(full, gain):
    values = full.astype(jnp.float32)
    mean_sq = jnp.mean(values * values, axis=-1, keepdims=True)
    return (values * lax.rsqrt(mean_sq + EPSILON) * gain).astype(jnp.bfloat16)


def attend(normed, weights_qkv, allowed):
    heads, hdim = (weights_qkv.shape[1], weights_qkv.shape[3])
    proj = jnp.einsum(
        "rd,dhtk->htrk", normed, weights_qkv, preferred_element_type=jnp.float32
    ).astype(jnp.bfloat16)

    def one_head(triple):
        query, keys, values = (triple[0], triple[1], triple[2])
        scores = jnp.dot(query, keys.T, preferred_element_type=jnp.float32) / math.sqrt(hdim)
        scores = jnp.where(allowed, scores, -1e30)
        probs = jnp.exp(scores - jnp.max(scores, axis=-1, keepdims=True))
        probs = (probs / jnp.sum(probs, axis=-1, keepdims=True)).astype(jnp.bfloat16)
        return jnp.dot(probs, values, preferred_element_type=jnp.float32).astype(jnp.bfloat16)

    mixed = lax.map(one_head, proj)
    return jnp.transpose(mixed, (1, 0, 2)).reshape(mixed.shape[1], heads * hdim)


def shards(
    tokens_in,
    patches,
    segment_ids,
    img_start,
    img_count,
    norm_gain,
    w_qkv,
    w_out,
    w_down1,
    w_down2,
    w_up1,
    w_up2,
    cotangent,
):
    n_section = lax.axis_size("section")
    section = lax.axis_index("section")
    final = n_section - 1
    micro, rows, width = tokens_in.shape
    img_tok = patches.shape[1]
    channels = w_down1.shape[1]
    qkv_full, out_full = (
        lax.all_gather(w_qkv, "dp", axis=1, tiled=True),
        lax.all_gather(w_out, "dp", axis=1, tiled=True),
    )
    qkv_layer = qkv_full[0]
    out_layer = out_full[0]
    gain = norm_gain[0]
    needs_down = section == 0

    def run_down(unused):
        return unet_down(patches, w_down1, w_down2)

    def no_down(unused):
        return (
            jnp.zeros((micro, img_tok, channels), jnp.bfloat16),
            jnp.zeros((micro, img_tok, width), jnp.bfloat16),
        )

    skipped, image_tokens = lax.cond(needs_down, run_down, no_down, 0)
    embedded = place_images(tokens_in, image_tokens, img_start, img_count)
    masks = jax.vmap(lambda seg, st, ct: allowed_pairs(seg, st, ct, rows, img_tok))(
        segment_ids, img_start, img_count
    )
    local_width = qkv_layer.shape[1] * qkv_layer.shape[3]

    def tick(carry, step):
        inbox, skip_box, outputs, kept = carry
        index = step - section
        live = (index >= 0) & (index < micro)
        slot = jnp.clip(index, 0, micro - 1)
        current = jnp.where(section == 0, lax.dynamic_index_in_dim(embedded, slot, 0, False), inbox)
        allowed = lax.dynamic_index_in_dim(masks, slot, 0, False)
        full = lax.all_gather(current, "tp", axis=1, tiled=True)

        def attend_live(unused):
            return attend(rms_normed(full, gain), qkv_layer, allowed)

        def attend_spare(unused):
            return jnp.zeros((rows, local_width), jnp.bfloat16)

        local_heads = lax.cond(live, attend_live, attend_spare, 0)
        all_heads = lax.all_gather(local_heads, "tp", axis=1, tiled=True)

        def project_live(unused):
            added = jnp.dot(all_heads, out_layer, preferred_element_type=jnp.float32)
            return (current.astype(jnp.float32) + added).astype(jnp.bfloat16)

        def project_spare(unused):
            return current

        result = lax.cond(live, project_live, project_spare, 0)
        previous = lax.dynamic_index_in_dim(outputs, slot, 0, False)
        outputs = lax.dynamic_update_index_in_dim(
            outputs, jnp.where(live, result, previous), slot, 0
        )
        outgoing = jnp.where(
            section == 0, lax.dynamic_index_in_dim(skipped, slot, 0, False), skip_box
        )
        stored = lax.dynamic_index_in_dim(kept, slot, 0, False)
        kept = lax.dynamic_update_index_in_dim(
            kept, jnp.where(live & (section == final), skip_box, stored), slot, 0
        )
        inbox, skip_box = passed_along((result, outgoing), "section", 1)
        return ((inbox, skip_box, outputs, kept), None)

    start_carry = (
        jnp.zeros((rows, width), jnp.bfloat16),
        jnp.zeros((img_tok, channels), jnp.bfloat16),
        jnp.zeros((micro, rows, width), jnp.bfloat16),
        jnp.zeros((micro, img_tok, channels), jnp.bfloat16),
    )
    ticks = micro + n_section - 1
    carry, unused = lax.scan(tick, start_carry, jnp.arange(ticks, dtype=jnp.int32))
    outputs = carry[2]
    skip_store = carry[3]
    final_rows = jax.vmap(lambda block, st: lax.dynamic_slice_in_dim(block, st, img_tok, 0))(
        outputs, img_start
    )
    partial_value = jnp.einsum("mkd,dc->mkc", final_rows, w_up1, preferred_element_type=jnp.float32)
    summed = lax.psum(partial_value.astype(jnp.bfloat16), "tp").astype(jnp.float32)
    upper = jax.nn.silu(summed + skip_store.astype(jnp.float32)).astype(jnp.bfloat16)
    upper = broadcast(upper, "section", final)
    present = (img_count > 0)[:, None, None]
    projected = jnp.einsum("mkc,cp->mkp", upper, w_up2, preferred_element_type=jnp.float32)
    image_pred = jnp.where(present, projected, 0.0).astype(jnp.bfloat16)
    weighted = jnp.where(present, cotangent, jnp.zeros_like(cotangent))
    grad_local = jnp.einsum("mkc,mkp->cp", upper, weighted, preferred_element_type=jnp.float32)
    grad_up = lax.psum(grad_local.astype(jnp.bfloat16), "dp").astype(jnp.float32)
    return (outputs[None], image_pred, grad_up)


def solution(mesh):
    placed = (
        P("dp", None, "tp"),
        P("dp", None, None),
        P("dp", None),
        P("dp"),
        P("dp"),
        P("section", None),
        P("section", "dp", "tp", None, None),
        P("section", "dp", "tp"),
        P(),
        P(None, "tp"),
        P("tp", None),
        P(None, "section"),
        P("dp", None, "section"),
    )
    return jax.shard_map(
        shards,
        mesh=mesh,
        in_specs=placed,
        out_specs=(P("section", "dp", None, "tp"), P("dp", None, "section"), P(None, "section")),
        check_vma=False,
    )
```

profile of v0, /device:TPU:0, one launch (start us, length us, event | category | flops | bytes accessed | tf_op | source)
XLA Modules:
  0.0 1289.1 jit_solution(7725941785170714117)
XLA Ops:
  7.2 3.3 copy.63
  13.1 3.4 conditional.3
  17.4 1.9 and_reduce_fusion
  19.3 3.1 select_select_fusion
  22.4 6.6 select_n.85
  29.1 174.4 %all-gather.7.cloned.1.call-done = bf16[1,2048,2048]{2,1,0:T(8,128)(2,1)} async-done(((bf16[1,64,2048]{2,1,0:T(8,128)(2,1)}), bf16[1,2048,2048]{2,1,0:T(8,128)(2,1)}) %all-gather.7.cloned.1.call-update) | async-done | bytes 8388624 | tf_op jit(solution)/shard_map/all_gather | solution.py:93
  203.5 536.5 %all-gather.5.cloned.1.call-done = bf16[1,4096,8,3,128]{4,1,3,2,0:T(8,128)(2,1)} async-done(((bf16[1,128,8,3,128]{4,1,3,2,0:T(8,128)(2,1)}), bf16[1,4096,8,3,128]{4,1,3,2,0:T(8,128)(2,1)}) %all-gather.5.cloned.1.call-update) | async-done | bytes 25165840 | tf_op jit(solution)/shard_map/all_gather | solution.py:92
  744.6 311.7 %while.30 = (s32[]{:T(128)}, bf16[512,2048]{1,0:T(8,128)(2,1)}, bf16[256,512]{1,0:T(8,128)(2,1)}, bf16[1,512,2048]{2,1,0:T(8,128)(2,1)}, bf16[1,256,512]{2,1,0:T...) while((s32[]{:T(128)}, bf16[512,2048]{1,0:T(8,128)(2,1)}, ...), condition=%wide.region_13.14_spmd.clone, body=%wide.region_3.13_spmd.clone.sunk | while | flops 17339318272 | bytes 138717024 | solution.py:163
  744.6 3.2 bitcast_select_fusion.5
  749.2 14.0 %all-gather.9.cloned.1.call-done = bf16[512,4096]{1,0:T(8,128)(2,1)} async-done(((bf16[512,2048]{1,0:T(8,128)(2,1)}), bf16[512,4096]{1,0:T(8,128)(2,1)}) %all-gather.9.cloned.1.call-update) | async-done | bytes 4194320 | tf_op jit(solution)/shard_map/while/body/eval_jaxpr/all_gather | solution.py:123
  764.4 53.1 %conditional.8 = (bf16[512,1024]{1,0:T(8,128)(2,1)S(1)}) conditional(s32[]{:T(128)} %convert_element_type.134, () %tuple.85, (bf16[512,4096]{1,0:T(8,128)(2,1)}, f32[1,4096]{1,0:T(1,128)S(1)}, bf16[4096,8,3,128]{3,0,2,1:T(8,128)(2,1)}, s32[512]{0:T(512)S(1)}, s32[1,512,512]{1,2,0:T(8,128)S(1)}, /*index=5*/s32[512]{0:T(512)S(1)}, ...), branch_computations={%region_4.4_spmd, %region_5.10_spmd} | conditional | flops 13038844928 | bytes 61908192 | solution.py:131
  764.4 3.2 fusion.12
  767.8 19.1 %convert_bitcast_fusion = bf16[8,3,512,128]{3,2,1,0:T(8,128)(2,1)} fusion(bf16[4096,8,3,128]{3,0,2,1:T(8,128)(2,1)} %get-tuple-element.178, bf16[512,4096]{1,0:T(8,128)(2,1)S(1)} %copy-done.1, f32[4096]{0:T(1024)S(1)} %bitcast.118, f32[512]{0:T(512)S(1)} %add_rsqrt_fusion), kind=kOutput, calls=%fused_computation.29 | convolution fusion | flops 12894863360 | bytes 32524288 | tf_op jit(solution)/shard_map/while/body/eval_jaxpr/cond/branch_1_fun/rd,dhtk->htrk/dot_general | solution.py:54
  788.5 27.5 %while.29 = (s32[]{:T(128)}, bf16[8,512,128]{2,1,0:T(8,128)(2,1)}, bf16[8,3,512,128]{3,2,1,0:T(8,128)(2,1)}, pred[512,512]{0,1:T(32,128)(4,1)S(1)}, s32[]{:T(128)}, /*index=5*/s32[]{:T(128)}, s32[]{}, s32[]{}) while((s32[]{:T(128)}, bf16[8,512,128]{2,1,0:T(8,128)(2,1)}, bf16[8,3,512,128]{3,2,1,0:T(8,128)(2,1)}, ...), condition=%wide.region_10.9_spmd, body=%wide.region_7.8_spmd.sunk | while | flops 136379392 | bytes 3944565 | solution.py:66
  810.7 1.9 fusion.61
  814.1 1.9 fusion.61
  818.5 13.3 %all-gather.11.cloned.1.call-done = bf16[512,2048]{1,0:T(8,128)(2,1)} async-done(((bf16[512,1024]{1,0:T(8,128)(2,1)}), bf16[512,2048]{1,0:T(8,128)(2,1)}) %all-gather.11.cloned.1.call-update) | async-done | bytes 2097168 | tf_op jit(solution)/shard_map/while/body/eval_jaxpr/all_gather | solution.py:132
  831.7 10.5 conditional.9
  831.7 10.5 add_convert_fusion
  842.2 2.6 collective-permute-start
  847.2 3.8 fusion.58
  850.9 44.0 %collective-permute-done.1 = bf16[256,512]{1,0:T(8,128)(2,1)S(1)} collective-permute-done((bf16[256,512]{1,0:T(8,128)(2,1)S(1)}, bf16[256,512]{1,0:T(8,128)(2,1)S(1)}, u32[]{:S(2)}, u32[]{:S(2)}) %collective-permute-start.1) | collective-permute-done | bytes 262176 | tf_op jit(solution)/shard_map/while/body/eval_jaxpr/ppermute | solution.py:14
  895.6 3.1 bitcast_select_fusion.5
  900.2 18.7 %all-gather.9.cloned.1.call-done = bf16[512,4096]{1,0:T(8,128)(2,1)} async-done(((bf16[512,2048]{1,0:T(8,128)(2,1)}), bf16[512,4096]{1,0:T(8,128)(2,1)}) %all-gather.9.cloned.1.call-update) | async-done | bytes 4194320 | tf_op jit(solution)/shard_map/while/body/eval_jaxpr/all_gather | solution.py:123
  921.3 67.7 %all-gather.11.cloned.1.call-done = bf16[512,2048]{1,0:T(8,128)(2,1)} async-done(((bf16[512,1024]{1,0:T(8,128)(2,1)}), bf16[512,2048]{1,0:T(8,128)(2,1)}) %all-gather.11.cloned.1.call-update) | async-done | bytes 2097168 | tf_op jit(solution)/shard_map/while/body/eval_jaxpr/all_gather | solution.py:132
  989.0 16.7 %collective-permute-start = (bf16[512,2048]{1,0:T(8,128)(2,1)}, bf16[512,2048]{1,0:T(8,128)(2,1)}, u32[]{:S(2)}, u32[]{:S(2)}) collective-permute-start(bf16[512,2048]{1,0:T(8,128)(2,1)} %get-tuple-element.540), channel_id=1, source_target_pairs={{0,64},{1,65},{2,66},{3,67},{4,68},{5,69},{6,70},{7,71},{8,72},{9,... | collective-permute-start | bytes 6291464 | tf_op jit(solution)/shard_map/while/body/eval_jaxpr/ppermute | solution.py:14
  1008.1 3.1 fusion.58
  1011.3 44.3 %collective-permute-done.1 = bf16[256,512]{1,0:T(8,128)(2,1)S(1)} collective-permute-done((bf16[256,512]{1,0:T(8,128)(2,1)S(1)}, bf16[256,512]{1,0:T(8,128)(2,1)S(1)}, u32[]{:S(2)}, u32[]{:S(2)}) %collective-permute-start.1) | collective-permute-done | bytes 262176 | tf_op jit(solution)/shard_map/while/body/eval_jaxpr/ppermute | solution.py:14
  1056.3 2.7 fusion.26
  1059.1 26.6 %all-reduce.3.cloned.1.call-done = bf16[1,256,512]{2,1,0:T(8,128)(2,1)} async-done(((bf16[1,256,512]{2,1,0:T(8,128)(2,1)}), bf16[1,256,512]{2,1,0:T(8,128)(2,1)}) %all-reduce.3.cloned.1.call-update) | async-done | bytes 262160 | tf_op jit(solution)/shard_map/psum | solution.py:170
  1087.5 33.4 %all-reduce.5.cloned.1.call-done = bf16[256,512]{1,0:T(8,128)(2,1)} async-done(((bf16[256,512]{1,0:T(8,128)(2,1)}), bf16[256,512]{1,0:T(8,128)(2,1)}) %all-reduce.5.cloned.1.call-update) | async-done | bytes 262160 | tf_op jit(solution)/shard_map/psum | solution.py:19
  1122.0 157.9 %psum.23 = bf16[512,16]{0,1:T(8,128)(2,1)S(1)} all-reduce(bf16[512,16]{0,1:T(8,128)(2,1)S(1)} %convolution_convert_fusion.3), channel_id=1, replica_groups=mesh['section'=2,'tp'=2,'dp'=32] {'dp'}, use_global_device_ids=true, to_apply=%region_16.17 | all-reduce | flops 8192 | bytes 32768 | tf_op jit(solution)/shard_map/psum | solution.py:178
  (120 shorter events, 54.5 us)
Async XLA Ops:
  7.2 1049.1 %copy-start = (bf16[2048,512]{1,0:T(8,128)(2,1)S(1)}, bf16[2048,512]{1,0:T(8,128)(2,1)}, u32[]{:S(2)}) copy-start(bf16[2048,512]{1,0:T(8,128)(2,1)} %param.35) | copy-start | bytes 6291460
  7.2 3.4 copy-start.10
  7.2 196.3 %all-gather.7.cloned.1.call-start = ((), (), s32[]{:S(2)}) async-start(), calls=%async_computation.1 | async-start | bytes 8650752 | tf_op jit(solution)/shard_map/all_gather | solution.py:93
  10.5 2.5 copy-start.16
  10.5 2.5 copy-start.17
  10.6 729.5 %all-gather.5.cloned.1.call-start = ((), (), s32[]{:S(2)}) async-start(), calls=%async_computation | async-start | bytes 25952256 | tf_op jit(solution)/shard_map/all_gather | solution.py:92
  13.1 3.4 copy-start.15
  13.1 4.3 copy-start.14
  13.1 1.7 copy-start.9
  16.5 2.8 copy-start.8
  740.0 4.6 copy-start.11
  740.0 4.6 copy-start.18
  744.6 18.6 %all-gather.9.cloned.1.call-start = ((), (), s32[]{:S(2)}) async-start(), calls=%async_computation.4 | async-start | bytes 6291456 | tf_op jit(solution)/shard_map/while/body/eval_jaxpr/all_gather | solution.py:123
  747.8 83.9 %all-gather.11.cloned.1.call-start = ((), (), s32[]{:S(2)}) async-start(), calls=%async_computation.5 | async-start | bytes 3145728 | tf_op jit(solution)/shard_map/while/body/eval_jaxpr/all_gather | solution.py:132
  764.4 3.4 copy-start.1
  831.7 13.0 %copy-start.3 = (bf16[1,256,512]{2,1,0:T(8,128)(2,1)S(1)}, bf16[1,256,512]{2,1,0:T(8,128)(2,1)}, u32[]{:S(2)}) copy-start(bf16[1,256,512]{2,1,0:T(8,128)(2,1)} %get-tuple-element.507) | copy-start | bytes 786436 | tf_op jit(solution)/shard_map/while
  831.7 13.0 %copy-start.6 = (bf16[256,512]{1,0:T(8,128)(2,1)S(1)}, bf16[256,512]{1,0:T(8,128)(2,1)}, u32[]{:S(2)}) copy-start(bf16[256,512]{1,0:T(8,128)(2,1)} %get-tuple-element.505) | copy-start | bytes 786436 | tf_op jit(solution)/shard_map/while
  842.2 52.7 %collective-permute-start = (bf16[512,2048]{1,0:T(8,128)(2,1)}, bf16[512,2048]{1,0:T(8,128)(2,1)}, u32[]{:S(2)}, u32[]{:S(2)}) collective-permute-start(bf16[512,2048]{1,0:T(8,128)(2,1)} %get-tuple-element.540), channel_id=1, source_target_pairs={{0,64},{1,65},{2,66},{3,67},{4,68},{5,69},{6,70},{7,71},{8,72},{9,... | collective-permute-start | bytes 6291464 | tf_op jit(solution)/shard_map/while/body/eval_jaxpr/ppermute | solution.py:14
  845.8 5.1 copy-start.4
  845.9 49.1 %collective-permute-start.1 = (bf16[256,512]{1,0:T(8,128)(2,1)S(1)}, bf16[256,512]{1,0:T(8,128)(2,1)S(1)}, u32[]{:S(2)}, u32[]{:S(2)}) collective-permute-start(bf16[256,512]{1,0:T(8,128)(2,1)S(1)} %get-tuple-element.449), channel_id=1, source_target_pairs={{0,64},{1,65},{2,66},{3,67},{4,68},{5,69},{6,70},{7,71},{8,72},{9,... | collective-permute-start | bytes 786440 | tf_op jit(solution)/shard_map/while/body/eval_jaxpr/ppermute | solution.py:14
  895.6 23.3 %all-gather.9.cloned.1.call-start = ((), (), s32[]{:S(2)}) async-start(), calls=%async_computation.4 | async-start | bytes 6291456 | tf_op jit(solution)/shard_map/while/body/eval_jaxpr/all_gather | solution.py:123
  898.8 90.2 %all-gather.11.cloned.1.call-start = ((), (), s32[]{:S(2)}) async-start(), calls=%async_computation.5 | async-start | bytes 3145728 | tf_op jit(solution)/shard_map/while/body/eval_jaxpr/all_gather | solution.py:132
  989.0 16.7 %copy-start.3 = (bf16[1,256,512]{2,1,0:T(8,128)(2,1)S(1)}, bf16[1,256,512]{2,1,0:T(8,128)(2,1)}, u32[]{:S(2)}) copy-start(bf16[1,256,512]{2,1,0:T(8,128)(2,1)} %get-tuple-element.507) | copy-start | bytes 786436 | tf_op jit(solution)/shard_map/while
  989.0 16.7 %copy-start.6 = (bf16[256,512]{1,0:T(8,128)(2,1)S(1)}, bf16[256,512]{1,0:T(8,128)(2,1)}, u32[]{:S(2)}) copy-start(bf16[256,512]{1,0:T(8,128)(2,1)} %get-tuple-element.505) | copy-start | bytes 786436 | tf_op jit(solution)/shard_map/while
  989.0 66.6 %collective-permute-start = (bf16[512,2048]{1,0:T(8,128)(2,1)}, bf16[512,2048]{1,0:T(8,128)(2,1)}, u32[]{:S(2)}, u32[]{:S(2)}) collective-permute-start(bf16[512,2048]{1,0:T(8,128)(2,1)} %get-tuple-element.540), channel_id=1, source_target_pairs={{0,64},{1,65},{2,66},{3,67},{4,68},{5,69},{6,70},{7,71},{8,72},{9,... | collective-permute-start | bytes 6291464 | tf_op jit(solution)/shard_map/while/body/eval_jaxpr/ppermute | solution.py:14
  1006.8 4.5 copy-start.4
  1006.8 48.8 %collective-permute-start.1 = (bf16[256,512]{1,0:T(8,128)(2,1)S(1)}, bf16[256,512]{1,0:T(8,128)(2,1)S(1)}, u32[]{:S(2)}, u32[]{:S(2)}) collective-permute-start(bf16[256,512]{1,0:T(8,128)(2,1)S(1)} %get-tuple-element.449), channel_id=1, source_target_pairs={{0,64},{1,65},{2,66},{3,67},{4,68},{5,69},{6,70},{7,71},{8,72},{9,... | collective-permute-start | bytes 786440 | tf_op jit(solution)/shard_map/while/body/eval_jaxpr/ppermute | solution.py:14
  1056.3 29.4 %copy-start.5 = (bf16[1,256,512]{2,1,0:T(8,128)(2,1)S(1)}, bf16[1,256,512]{2,1,0:T(8,128)(2,1)}, u32[]{:S(2)}) copy-start(bf16[1,256,512]{2,1,0:T(8,128)(2,1)} %get-tuple-element.210) | copy-start | bytes 786436
  1056.3 29.4 %all-reduce.3.cloned.1.call-start = ((), (), s32[]{:S(2)}) async-start(), calls=%async_computation.2 | async-start | bytes 524288 | tf_op jit(solution)/shard_map/psum | solution.py:170
  1056.3 64.6 %copy-start.13 = (bf16[1,256,16]{1,2,0:T(8,128)(2,1)S(1)}, bf16[1,256,16]{1,2,0:T(8,128)(2,1)}, u32[]{:S(2)}) copy-start(bf16[1,256,16]{1,2,0:T(8,128)(2,1)} %param.37) | copy-start | bytes 24580
  1056.3 224.2 %copy-start.12 = (bf16[512,16]{0,1:T(8,128)(2,1)S(1)}, bf16[512,16]{0,1:T(8,128)(2,1)}, u32[]{:S(2)}) copy-start(bf16[512,16]{0,1:T(8,128)(2,1)} %param.36) | copy-start | bytes 49156
  1059.0 61.8 %all-reduce.5.cloned.1.call-start = ((), (), s32[]{:S(2)}) async-start(), calls=%async_computation.3 | async-start | bytes 524288 | tf_op jit(solution)/shard_map/psum | solution.py:19
  (4 other events, 3.4 us)
Sparse Core Ops, SparseCore 0:
  10.7 192.7 all-gather.6
  205.1 534.8 all-gather.4
  747.9 15.2 all-gather.8
  818.6 13.0 all-gather.10
  898.9 19.9 all-gather.8
  921.4 67.5 all-gather.10
  1059.6 26.0 all-reduce.2
  1088.2 32.6 all-reduce.4
where the time goes:
time: 1290 us
  waiting for transfers between devices  973 us (75%)
  blocking collectives  158 us (12%)
  matrix products  63.7 us (5%)
  other arithmetic  29.3 us (2%)
  local copies, waits for them, and re-layouts  25.9 us (2%)
  starting transfers between devices  22.1 us (2%)
  between operations  15.5 us (1%)
    all_gather x1, waiting for transfers between devices, shards(): lax.all_gather(w_qkv, 'dp', axis=1, tiled=True)  537 us
    all_gather x1, waiting for transfers between devices, shards(): lax.all_gather(w_out, 'dp', axis=1, tiled=True)  174 us
    psum x1, blocking collectives, shards(): lax.psum(grad_local.astype(jnp.bfloat16), 'dp').astype(jnp.float32)  158 us
    ppermute x4, waiting for transfers between devices, passed_along(): return lax.ppermute(value, axis, pairs)  88.3 us
    all_gather x2, waiting for transfers between devices, tick(): all_heads = lax.all_gather(local_heads, 'tp', axis=1, tiled=True)  81 us
    psum x1, waiting for transfers between devices, broadcast(): return lax.psum(block, axis)  33.4 us
    all_gather x2, waiting for transfers between devices, tick(): full = lax.all_gather(current, 'tp', axis=1, tiled=True)  32.7 us
    psum x1, waiting for transfers between devices, shards(): lax.psum(partial_value.astype(jnp.bfloat16), 'tp').astype(jnp.float32)  26.6 us
  transfers between devices with their start and end apart: 12, of which 10 were waited for; matrix products, arithmetic and copies ran while one was open for 2% of the time, Pallas kernels for 0%

commit v1 on v0

v1 whole, which is shorter than its diff:
```python
import functools
import math

import jax
import jax.numpy as jnp
from jax import lax
from jax.experimental import pallas as pl
from jax.experimental.pallas import tpu as pltpu
from jax.sharding import PartitionSpec as P

EPSILON = 1e-05
MESH = pl.DeviceIdType.MESH
ANY = pl.BlockSpec(memory_space=pl.ANY)
VM = pl.BlockSpec(memory_space=pltpu.VMEM)
RING = 4


class Place:
    def __init__(self):
        self.s = lax.axis_index("section")
        self.c = lax.axis_index("tp")
        d = lax.axis_index("dp")
        self.k = lax.rem(d, 2)
        self.y = lax.rem(lax.div(d, 2), RING)
        self.z = lax.div(d, 2 * RING)
        self.x = 2 * self.s + self.k

    def at(self, dx=0, dy=0, dz=0, sibling=False):
        x = lax.rem(self.x + dx, RING)
        y = lax.rem(self.y + dy, RING)
        z = lax.rem(self.z + dz, RING)
        return {
            "section": lax.div(x, 2),
            "tp": 1 - self.c if sibling else self.c,
            "dp": z * 8 + y * 2 + lax.rem(x, 2),
        }


def greet(peers):
    barrier = pltpu.get_barrier_semaphore()
    for peer in peers:
        pl.semaphore_signal(barrier, inc=1, device_id=peer, device_id_type=MESH)
    pl.semaphore_wait(barrier, len(peers))


def remote(src, dst, send, recv, peer):
    return pltpu.make_async_remote_copy(
        src_ref=src, dst_ref=dst, send_sem=send, recv_sem=recv, device_id=peer, device_id_type=MESH
    )


def gather_kernel(
    wq, wo, xin, gain, meta, q_all, o_all, x_all, g_all, m_all, s0, r0, s1, r1, s2, r2, sx, rx, loc
):
    me = Place()
    s, c, k, x, y, z = me.s, me.c, me.k, me.x, me.y, me.z
    greet([me.at(dx=j) for j in (1, 2, 3)] + [me.at(dy=1), me.at(dy=3), me.at(dz=1), me.at(dz=3)]
          + [me.at(sibling=True)])
    pending = []
    for a, (src, dst) in enumerate(((wq, q_all), (wo, o_all))):
        for j in (1, 2, 3):
            peer_x = lax.rem(x + j, RING)
            cp = remote(src.at[peer_x], dst.at[s, z, y, k], s0.at[a, j], r0.at[a, x], me.at(dx=j))
            cp.start()
            pending.append(cp)
        pltpu.make_async_copy(src.at[x], dst.at[s, z, y, k], r0.at[a, x]).start()
    width = xin.shape[1]
    half = xin.shape[0] // 2
    cols = pl.ds(pl.multiple_of(c * width, width), width)
    x_loc = pltpu.make_async_copy(xin, x_all.at[k, :, cols], loc.at[0])
    g_loc = pltpu.make_async_copy(gain, g_all.at[s], loc.at[1])
    m_loc = pltpu.make_async_copy(meta, m_all.at[k], loc.at[2])
    for cp in (x_loc, g_loc, m_loc):
        cp.start()
    low, high = pl.ds(0, half), pl.ds(half, half)
    up = remote(xin.at[low], x_all.at[k, low, cols], sx.at[0], rx.at[0], me.at(dx=1))
    down = remote(xin.at[high], x_all.at[k, high, cols], sx.at[1], rx.at[1], me.at(dx=3))
    side = remote(xin, x_all.at[k, :, cols], sx.at[2], rx.at[2], me.at(sibling=True))
    g_cp = remote(gain, g_all.at[s], sx.at[3], rx.at[3], me.at(dx=2))
    m_cp = remote(meta, m_all.at[k], sx.at[4], rx.at[4], me.at(dx=1))
    for cp in (up, down, side, g_cp, m_cp):
        cp.start()

    def spot(ref, layer, kk, zz, yy, rows=None):
        view = ref.at[layer, zz, yy, kk]
        return view if rows is None else view.at[rows]

    items = [(layer, kk) for layer in (0, 1) for kk in (0, 1)]
    ring1 = {}
    for i, (layer, kk) in enumerate(items):
        for a, ref in enumerate((q_all, o_all)):
            own = spot(ref, layer, kk, z, y)
            pltpu.make_async_copy(own, own, r0.at[a, i]).wait()
            for direction in (0, 1):
                step = 1 if direction == 0 else 3
                peer = me.at(dy=step) if kk == 0 else me.at(dz=step)
                cp = remote(own, own, s1.at[a, i, direction], r1.at[a, i, direction], peer)
                cp.start()
                ring1[a, i, direction] = cp
    for i, (layer, kk) in enumerate(items):
        for a, ref in enumerate((q_all, o_all)):
            rows = ref.shape[4]
            for direction in (0, 1):
                step = 1 if direction == 0 else 3
                ring1[a, i, direction].wait_recv()
                zz = z if kk == 0 else lax.rem(z + 4 - step, RING)
                yy = lax.rem(y + 4 - step, RING) if kk == 0 else y
                part = spot(ref, layer, kk, zz, yy, pl.ds(direction * rows // 2, rows // 2))
                peer = me.at(dy=step) if kk == 0 else me.at(dz=step)
                cp = remote(part, part, s1.at[a, i, 2 + direction], r1.at[a, i, 2 + direction], peer)
                cp.start()
                ring1[a, i, 2 + direction] = cp
    ring2 = {}

    def band(ref, layer, kk, zz, yy, part=None):
        if part is None:
            return ref.at[layer, zz, :, kk] if kk == 0 else ref.at[layer, :, yy, kk]
        piece = pl.ds(2 * part, 2)
        return ref.at[layer, zz, piece, kk] if kk == 0 else ref.at[layer, piece, yy, kk]

    for i, (layer, kk) in enumerate(items):
        for a, ref in enumerate((q_all, o_all)):
            for direction in (0, 1):
                ring1[a, i, 2 + direction].wait_recv()
            own = band(ref, layer, kk, z, y)
            for direction in (0, 1):
                step = 1 if direction == 0 else 3
                peer = me.at(dz=step) if kk == 0 else me.at(dy=step)
                cp = remote(own, own, s2.at[a, i, direction], r2.at[a, i, direction], peer)
                cp.start()
                ring2[a, i, direction] = cp
    other = 1 - k
    up.wait_recv()
    side_low = remote(x_all.at[other, low, cols], x_all.at[other, low, cols], sx.at[5], rx.at[5],
                      me.at(sibling=True))
    side_low.start()
    down.wait_recv()
    side_high = remote(x_all.at[other, high, cols], x_all.at[other, high, cols], sx.at[6], rx.at[6],
                       me.at(sibling=True))
    side_high.start()
    for i, (layer, kk) in enumerate(items):
        for a, ref in enumerate((q_all, o_all)):
            for direction in (0, 1):
                step = 1 if direction == 0 else 3
                ring2[a, i, direction].wait_recv()
                zz = lax.rem(z + 4 - step, RING) if kk == 0 else z
                yy = y if kk == 0 else lax.rem(y + 4 - step, RING)
                part = band(ref, layer, kk, zz, yy, direction)
                peer = me.at(dz=step) if kk == 0 else me.at(dy=step)
                cp = remote(part, part, s2.at[a, i, 2 + direction], r2.at[a, i, 2 + direction], peer)
                cp.start()
                ring2[a, i, 2 + direction] = cp
    for key, cp in ring2.items():
        if key[2] >= 2:
            cp.wait_recv()
    for cp in (side, g_cp, m_cp, side_low, side_high):
        cp.wait_recv()
    for cp in (x_loc, g_loc, m_loc):
        cp.wait()
    for cp in pending + [up, down, side, g_cp, m_cp, side_low, side_high]:
        cp.wait_send()
    for cp in list(ring1.values()) + list(ring2.values()):
        cp.wait_send()


def gather_inputs(wq, wo, xin, gain, meta):
    bf16 = jnp.bfloat16
    rows_q, wide_q = wq.shape[1:]
    rows_o, wide_o = wo.shape[1:]
    dma = pltpu.SemaphoreType.DMA
    return pl.pallas_call(
        gather_kernel,
        out_shape=(
            jax.ShapeDtypeStruct((2, 4, 4, 2, rows_q, wide_q), bf16),
            jax.ShapeDtypeStruct((2, 4, 4, 2, rows_o, wide_o), bf16),
            jax.ShapeDtypeStruct((2, xin.shape[0], 2 * xin.shape[1]), bf16),
            jax.ShapeDtypeStruct((2,) + gain.shape, jnp.float32),
            jax.ShapeDtypeStruct((2,) + meta.shape, jnp.int32),
        ),
        in_specs=[ANY] * 5,
        out_specs=(ANY,) * 5,
        scratch_shapes=[
            dma((2, 4)), dma((2, 4)), dma((2, 4, 4)), dma((2, 4, 4)), dma((2, 4, 4)), dma((2, 4, 4)),
            dma((7,)), dma((7,)), dma((3,)),
        ],
        compiler_params=pltpu.CompilerParams(collective_id=0, has_side_effects=True),
        name="gather_inputs",
    )(wq, wo, xin, gain, meta)


def ring_kernel(v, v_all, ss, rs, loc):
    me = Place()
    c, x = me.c, me.x
    greet([me.at(dx=1), me.at(dx=3), me.at(sibling=True)])
    rows, width = v.shape
    half = rows // 2

    def cols(xx):
        start = (c * RING + xx) * width
        return pl.ds(pl.multiple_of(start, width), width)

    low, high = pl.ds(0, half), pl.ds(half, half)
    mine = v_all.at[:, cols(x)]
    local = pltpu.make_async_copy(v, mine, loc)
    local.start()
    up = remote(v, mine, ss.at[0], rs.at[0], me.at(dx=1))
    down = remote(v, mine, ss.at[1], rs.at[1], me.at(dx=3))
    side = remote(v, mine, ss.at[2], rs.at[2], me.at(sibling=True))
    for cp in (up, down, side):
        cp.start()
    left, right, far = (lax.rem(x + j, RING) for j in (3, 1, 2))
    copies = [up, down, side]

    def forward(part, index, peer):
        cp = remote(part, part, ss.at[index], rs.at[index], peer)
        cp.start()
        copies.append(cp)
        return cp

    up.wait_recv()
    on_up = forward(v_all.at[low, cols(left)], 3, me.at(dx=1))
    waits = [side, forward(v_all.at[:, cols(left)], 5, me.at(sibling=True))]
    down.wait_recv()
    on_down = forward(v_all.at[high, cols(right)], 4, me.at(dx=3))
    waits.append(forward(v_all.at[:, cols(right)], 6, me.at(sibling=True)))
    on_up.wait_recv()
    waits.append(forward(v_all.at[low, cols(far)], 7, me.at(sibling=True)))
    on_down.wait_recv()
    waits.append(forward(v_all.at[high, cols(far)], 8, me.at(sibling=True)))
    for cp in waits:
        cp.wait_recv()
    for cp in copies:
        cp.wait_send()
    local.wait()


def ring_gather(v, ident):
    rows, width = v.shape
    dma = pltpu.SemaphoreType.DMA
    return pl.pallas_call(
        ring_kernel,
        out_shape=jax.ShapeDtypeStruct((rows, 8 * width), v.dtype),
        in_specs=[ANY],
        out_specs=ANY,
        scratch_shapes=[dma((9,)), dma((9,)), dma],
        compiler_params=pltpu.CompilerParams(collective_id=ident, has_side_effects=True),
        name="ring_gather",
    )(v)


def tail_kernel(part, skipped, w_up2, weighted, pred, grad, got, pair, ys, zs, sem_s, sem_r):
    me = Place()
    partner = {"section": me.s, "tp": me.c, "dp": me.z * 8 + me.y * 2 + 1 - me.k}
    peers_y = [me.at(dy=j) for j in (1, 2, 3)]
    peers_z = [me.at(dz=j) for j in (1, 2, 3)]
    greet([me.at(sibling=True), partner] + peers_y + peers_z)
    cp = remote(part, got, sem_s.at[0], sem_r.at[0], me.at(sibling=True))
    cp.start()
    cp.wait()
    summed = part[...].astype(jnp.float32) + got[...].astype(jnp.float32)
    value = summed + skipped[...].astype(jnp.float32)
    upper = (value / (1.0 + jnp.exp(-value))).astype(jnp.bfloat16)
    pred[...] = jnp.dot(upper, w_up2[...], preferred_element_type=jnp.float32)
    g0 = lax.dot_general(weighted[...], upper, (((0,), (0,)), ((), ())),
                         preferred_element_type=jnp.float32)
    pair[0] = g0
    cp = remote(pair.at[0], pair.at[1], sem_s.at[1], sem_r.at[1], partner)
    cp.start()
    cp.wait()
    ys[me.y] = pair[0] + pair[1]
    copies = []
    for n, peer in enumerate(peers_y):
        cp = remote(ys.at[me.y], ys.at[me.y], sem_s.at[2 + n], sem_r.at[2 + n], peer)
        cp.start()
        copies.append(cp)
    for cp in copies:
        cp.wait()
    zs[me.z] = ys[0] + ys[1] + ys[2] + ys[3]
    copies = []
    for n, peer in enumerate(peers_z):
        cp = remote(zs.at[me.z], zs.at[me.z], sem_s.at[5 + n], sem_r.at[5 + n], peer)
        cp.start()
        copies.append(cp)
    for cp in copies:
        cp.wait()
    grad[...] = zs[0] + zs[1] + zs[2] + zs[3]


def unet_tail(part, skipped, w_up2, weighted):
    rows, channels = part.shape
    wide = w_up2.shape[1]
    f32 = jnp.float32
    dma = pltpu.SemaphoreType.DMA
    return pl.pallas_call(
        tail_kernel,
        out_shape=(jax.ShapeDtypeStruct((rows, wide), f32), jax.ShapeDtypeStruct((wide, channels), f32)),
        in_specs=[VM] * 4,
        out_specs=(VM, VM),
        scratch_shapes=[
            pltpu.VMEM(part.shape, part.dtype),
            pltpu.VMEM((2, wide, channels), f32),
            pltpu.VMEM((4, wide, channels), f32),
            pltpu.VMEM((4, wide, channels), f32),
            dma((8,)), dma((8,)),
        ],
        compiler_params=pltpu.CompilerParams(collective_id=5, has_side_effects=True,
                                             vmem_limit_bytes=32 << 20),
        name="unet_tail",
    )(part, skipped, w_up2, weighted)


def allowed_pairs(meta, rows, img_tok):
    segment, start, count = meta[0], meta[1, :1], meta[2, :1]
    position = jnp.arange(rows, dtype=jnp.int32)
    in_image = (count > 0) & (position >= start) & (position < start + img_tok)
    same = segment[:, None] == segment[None, :]
    causal = position[None, :] <= position[:, None]
    return same & (causal | in_image[:, None] & in_image[None, :])


def shards(
    tokens_in, patches, segment_ids, img_start, img_count, norm_gain, w_qkv, w_out, w_down1, w_down2,
    w_up1, w_up2, cotangent,
):
    bf16, f32 = jnp.bfloat16, jnp.float32
    me = Place()
    rows, width = tokens_in.shape[1:]
    img_tok = patches.shape[1]
    depth, heads, three, hdim = w_qkv.shape[1:]
    per = heads // RING
    wide_q = per * three * hdim
    out_cols = w_out.shape[2] // RING
    wq = jnp.transpose(w_qkv[0].reshape(depth, RING, wide_q), (1, 0, 2))
    wo = jnp.transpose(w_out[0].reshape(w_out.shape[1], RING, out_cols), (1, 0, 2))

    inner = jnp.dot(patches[0], w_down1, preferred_element_type=f32)
    skipped = jax.nn.silu(inner).astype(bf16)
    image = jnp.dot(skipped, w_down2, preferred_element_type=f32).astype(bf16)
    placed = lax.dynamic_update_slice_in_dim(tokens_in[0], image, img_start[0], 0)
    x_own = jnp.where(img_count[0] > 0, placed, tokens_in[0])
    meta = jnp.concatenate(
        [segment_ids, jnp.broadcast_to(img_start[:, None], (1, rows)),
         jnp.broadcast_to(img_count[:, None], (1, rows)), jnp.zeros((5, rows), jnp.int32)], axis=0)

    q_all, o_all, x_all, gains, metas = gather_inputs(wq, wo, x_own, norm_gain, meta)
    allowed = jax.vmap(lambda m: allowed_pairs(m, rows, img_tok))(metas)
    current = x_all.reshape(2 * rows, 2 * width)
    first = (me.c * RING + me.x) * out_cols
    states = []
    for layer in (0, 1):
        weights = q_all[layer].reshape(-1, wide_q)
        values = current.astype(f32)
        mean_sq = jnp.mean(values * values, axis=-1, keepdims=True)
        normed = (values * lax.rsqrt(mean_sq + EPSILON) * gains[layer]).astype(bf16)
        proj = jnp.dot(normed, weights, preferred_element_type=f32).astype(bf16)
        proj = proj.reshape(2, rows, per, three, hdim)
        query, keys, vals = proj[:, :, :, 0], proj[:, :, :, 1], proj[:, :, :, 2]
        scores = jnp.einsum("mqhk,mshk->mhqs", query, keys, preferred_element_type=f32) / math.sqrt(hdim)
        scores = jnp.where(allowed[:, None], scores, -1e30)
        probs = jnp.exp(scores - jnp.max(scores, axis=-1, keepdims=True))
        probs = (probs / jnp.sum(probs, axis=-1, keepdims=True)).astype(bf16)
        mixed = jnp.einsum("mhqs,mshk->mqhk", probs, vals, preferred_element_type=f32).astype(bf16)
        all_heads = ring_gather(mixed.reshape(2 * rows, per * hdim), 1 + layer)
        added = jnp.dot(all_heads, o_all[layer].reshape(-1, out_cols), preferred_element_type=f32)
        mine = lax.dynamic_slice_in_dim(current, first, out_cols, 1)
        result = (mine.astype(f32) + added).astype(bf16)
        current = ring_gather(result, 3 + layer if layer == 0 else 4)
        states.append(current)

    def own_block(full):
        return lax.dynamic_slice(full, (me.k * rows, me.c * width), (rows, width))

    hidden = jnp.where(me.s == 0, own_block(states[0]), own_block(states[1]))
    final = lax.dynamic_slice(states[1], (me.k * rows + img_start[0], me.c * width), (img_tok, width))
    part = jnp.dot(final, w_up1, preferred_element_type=f32)
    weighted = jnp.where(img_count[0] > 0, cotangent[0], jnp.zeros_like(cotangent[0]))
    pred, grad = unet_tail(part, skipped, w_up2, weighted)
    pred = jnp.where(img_count[0] > 0, pred, 0.0).astype(bf16)
    return (hidden[None, None], pred[None], grad.T)


def solution(mesh):
    placed = (
        P("dp", None, "tp"),
        P("dp", None, None),
        P("dp", None),
        P("dp"),
        P("dp"),
        P("section", None),
        P("section", "dp", "tp", None, None),
        P("section", "dp", "tp"),
        P(),
        P(None, "tp"),
        P("tp", None),
        P(None, "section"),
        P("dp", None, "section"),
    )
    return jax.shard_map(
        shards,
        mesh=mesh,
        in_specs=placed,
        out_specs=(P("section", "dp", None, "tp"), P("dp", None, "section"), P(None, "section")),
        check_vma=False,
    )
```

time: 1290 us -> 381 us (0.30)
  waiting for transfers between devices: 973 us -> 0 us
  Pallas kernels: 0 us -> 258 us
  blocking collectives: 158 us -> 0 us
  local copies, waits for them, and re-layouts: 25.9 us -> 50.4 us
  matrix products: 63.7 us -> 40 us
  starting transfers between devices: 22.1 us -> 0 us
  between operations: 15.5 us -> 2.38 us
    all_gather x6 -> x0, waiting for transfers between devices: 825 us -> none  [the longest x1 537 us: shards(): lax.all_gather(w_qkv, 'dp', axis=1, tiled=True)]
    pallas_call x0 -> x6, Pallas kernels: none -> 258 us  [the longest x4 137 us: ring_gather(): pl.pallas_call(ring_kernel, out_shape=jax.ShapeDtypeStruct((rows, 8 * wid...]
    psum x1 -> x0, blocking collectives: 158 us -> none  [shards(): lax.psum(grad_local.astype(jnp.bfloat16), 'dp').astype(jnp.float32)]
    ppermute x4 -> x0, waiting for transfers between devices: 88.3 us -> none  [passed_along(): return lax.ppermute(value, axis, pairs)]
    psum x2 -> x0, waiting for transfers between devices: 59.9 us -> none  [the longest x1 33.4 us: broadcast(): return lax.psum(block, axis)]
    dot_general x23 -> x11, matrix products: 63.7 us -> 40 us  [the longest x2 20.5 us: shards(): proj = jnp.dot(normed, weights, preferred_element_type=f32).astype(bf16)]
    ppermute x4 -> x0, starting transfers between devices: 21.9 us -> none  [passed_along(): return lax.ppermute(value, axis, pairs)]
    slice x0 -> x7, local copies, waits for them, and re-layouts: none -> 21.1 us  [the longest x1 11.7 us: shards(): weights = q_all[layer].reshape(-1, wide_q)]
  transfers between devices with their start and end apart: 12 -> 0, of which waited for: 10 -> 0; matrix products, arithmetic and copies ran while one was open for 2% -> 0% of each run, Pallas kernels for 0% -> 0%
where the time goes in v1:
time: 381 us; the launch traced here: 380 us
  Pallas kernels  258 us (68%)
  local copies, waits for them, and re-layouts  50.4 us (13%)
  matrix products  40 us (10%)
  other arithmetic  29.1 us (8%)
    pallas_call x4, Pallas kernels, ring_gather(): pl.pallas_call(ring_kernel, out_shape=jax.ShapeDtypeStruct((rows, 8 * wid...  137 us
    pallas_call x1, Pallas kernels, gather_inputs(): pl.pallas_call(gather_kernel, out_shape=(jax.ShapeDtypeStruct((2, 4, 4, 2...  105 us
    dot_general x2, matrix products, shards(): proj = jnp.dot(normed, weights, preferred_element_type=f32).astype(bf16)  20.5 us
    pallas_call x1, Pallas kernels, unet_tail(): pl.pallas_call(tail_kernel, out_shape=(jax.ShapeDtypeStruct((rows, wide),...  15.7 us
    dot_general x2, matrix products, shards(): jnp.dot(all_heads, o_all[layer].reshape(-1, out_cols), preferred_element_...  12.2 us
    slice x1, local copies, waits for them, and re-layouts, shards(): weights = q_all[layer].reshape(-1, wide_q)  11.7 us
    unnamed x41, local copies, waits for them, and re-layouts  11 us
    convert_element_type x1, other arithmetic, shards(): normed = (values * lax.rsqrt(mean_sq + EPSILON) * gains[layer]).astype(bf16)  10.3 us

profile of v1, /device:TPU:0, one launch (start us, length us, event | category | flops | bytes accessed | tf_op | source)
XLA Modules:
  0.0 379.8 jit_solution(8296038173553136635)
XLA Ops:
  0.7 3.3 copy.75
  4.0 1.6 copy.29
  5.6 1.2 copy.30
  9.4 2.0 fusion.14
  11.4 5.9 %select_n.70.xin = bf16[512,2048]{1,0:T(8,128)(2,1)} dynamic-update-slice(bf16[512,2048]{1,0:T(8,128)(2,1)} %bitcast.87, bf16[256,2048]{1,0:T(8,128)(2,1)S(1)} %fusion.14, s32[]{:T(128)S(6)} %select_n.66, s32[]{:T(128)} %constant.14.clone.1) | dynamic-update-slice | bytes 2097156 | tf_op jit(solution)/shard_map/jit(_where)/select_n | solution.py:340
  18.2 104.7 %gather_inputs.1 = (bf16[2,4,4,2,128,768]{5,4,3,2,1,0:T(8,128)(2,1)}, bf16[2,4,4,2,64,512]{5,4,3,2,1,0:T(8,128)(2,1)}, bf16[2,512,4096]{2,1,0:T(8,128)(2,1)}, f32[2,1,4096]{2,1,0:T(1,128)}, s32[2,8,512]{2,1,0:T(8,128)}) custom-call(bf16[4,128,768]{2,1,0:T(8,128)(2,1)} %bitcast.92, bf16[4,64,512]{2,1,0:T(8,128)(2,1)} %bitcast.99, ...), custom_call_target="tpu_custom_call" | custom-call | tf_op jit(solution)/shard_map/gather_inputs/pallas_call | solution.py:171
  123.0 11.7 %fusion.44 = (bf16[1,4,4,2,128,768]{5,4,3,2,1,0:T(8,128)(2,1)}, bf16[1,4,4,2,128,768]{5,4,3,2,1,0:T(8,128)(2,1)}) fusion(bf16[2,4,4,2,128,768]{5,4,3,2,1,0:T(8,128)(2,1)} %get-tuple-element.12), kind=kLoop, calls=%fused_computation.74 | loop fusion | bytes 25165824 | tf_op jit(solution)/shard_map/slice | solution.py:351
  134.6 1.7 fusion.2
  136.4 10.3 %fusion.4 = bf16[2,512,4096]{2,1,0:T(8,128)(2,1)} fusion(bf16[2,512,4096]{2,1,0:T(8,128)(2,1)} %get-tuple-element.10, f32[4096]{0:T(1024)S(1)} %bitcast.100, f32[2,512]{1,0:T(2,128)S(1)} %add_rsqrt_fusion.1), kind=kLoop, calls=%fused_computation.8 | loop fusion | flops 16777216 | bytes 16797696 | tf_op jit(solution)/shard_map/convert_element_type | solution.py:354
  146.7 10.9 %convolution_convert_fusion.1 = bf16[1024,768]{1,0:T(8,128)(2,1)S(1)} fusion(bf16[1024,4096]{1,0:T(8,128)(2,1)} %bitcast.88, bf16[4096,768]{1,0:T(8,128)(2,1)} %bitcast.90), kind=kOutput, calls=%fused_computation.38 | convolution fusion | flops 6443237376 | bytes 16252928 | tf_op jit(solution)/shard_map/dot_general | solution.py:355
  157.6 1.6 copy.32
  159.2 2.9 reshape.210
  162.1 1.9 fusion.47
  169.1 2.4 fusion.49
  172.5 0.9 copy.67
  173.3 26.0 %ring_gather.4 = bf16[1024,2048]{1,0:T(8,128)(2,1)} custom-call(bf16[1024,256]{1,0:T(8,128)(2,1)} %bitcast.93), custom_call_target="tpu_custom_call" | custom-call | tf_op jit(solution)/shard_map/ring_gather/pallas_call | solution.py:240
  199.4 4.0 %fusion.45 = (bf16[1,4,4,2,64,512]{5,4,3,2,1,0:T(8,128)(2,1)}, bf16[1,4,4,2,64,512]{5,4,3,2,1,0:T(8,128)(2,1)S(1)}) fusion(bf16[2,4,4,2,64,512]{5,4,3,2,1,0:T(8,128)(2,1)} %get-tuple-element.14), kind=kLoop, calls=%fused_computation.75 | loop fusion | bytes 8388608 | tf_op jit(solution)/shard_map/slice | solution.py:364
  203.4 5.9 %add_convert_fusion.1.v = bf16[1024,512]{1,0:T(8,128)(2,1)} fusion(bf16[1024,2048]{1,0:T(8,128)(2,1)} %ring_gather.4, bf16[2048,512]{1,0:T(8,128)(2,1)S(1)} %bitcast.98, bf16[1024,4096]{1,0:T(8,128)(2,1)} %bitcast.84, s32[]{:T(128)S(6)} %select_n.71), kind=kOutput, calls=%fused_computation.27 | convolution fusion | flops 2149056512 | bytes 8388612 | tf_op jit(solution)/shard_map/dot_general | solution.py:364
  209.3 43.9 %ring_gather.5 = bf16[1024,4096]{1,0:T(8,128)(2,1)} custom-call(bf16[1024,512]{1,0:T(8,128)(2,1)} %add_convert_fusion.1.v), custom_call_target="tpu_custom_call" | custom-call | tf_op jit(solution)/shard_map/ring_gather/pallas_call | solution.py:240
  253.2 5.2 %fusion.5 = f32[1024]{0:T(1024)S(1)} fusion(bf16[1024,4096]{1,0:T(8,128)(2,1)} %ring_gather.5), kind=kLoop, calls=%fused_computation.9 | loop fusion | flops 12581888 | bytes 8392704 | tf_op jit(solution)/shard_map/reduce_sum | solution.py:353
  259.0 9.6 %fusion.23 = bf16[1024,768]{1,0:T(8,128)(2,1)S(1)} fusion(bf16[4096,768]{1,0:T(8,128)(2,1)} %bitcast.89, bf16[1024,4096]{1,0:T(8,128)(2,1)S(1)} %copy-done.2, f32[4096]{0:T(1024)S(1)} %bitcast.102, f32[1024]{0:T(1024)S(1)} %add_rsqrt_fusion), kind=kOutput, calls=%fused_computation.37 | convolution fusion | flops 6460014592 | bytes 16273408 | tf_op jit(solution)/shard_map/dot_general | solution.py:355
  268.5 1.7 copy.38
  270.2 3.1 reshape.212
  273.3 1.9 fusion.46
  276.9 2.4 fusion.50
  280.3 0.9 copy.66
  281.2 24.0 %ring_gather.6 = bf16[1024,2048]{1,0:T(8,128)(2,1)} custom-call(bf16[1024,256]{1,0:T(8,128)(2,1)} %bitcast.94), custom_call_target="tpu_custom_call" | custom-call | tf_op jit(solution)/shard_map/ring_gather/pallas_call | solution.py:240
  305.2 6.4 %add_convert_fusion.v = bf16[1024,512]{1,0:T(8,128)(2,1)} fusion(bf16[1024,2048]{1,0:T(8,128)(2,1)} %ring_gather.6, bf16[2048,512]{1,0:T(8,128)(2,1)} %bitcast.97, bf16[1024,4096]{1,0:T(8,128)(2,1)} %ring_gather.5, s32[]{:T(128)S(6)} %select_n.71), kind=kOutput, calls=%fused_computation.26 | convolution fusion | flops 2149056512 | bytes 8388612 | tf_op jit(solution)/shard_map/dot_general | solution.py:364
  311.5 43.5 %ring_gather.7 = bf16[1024,4096]{1,0:T(8,128)(2,1)} custom-call(bf16[1024,512]{1,0:T(8,128)(2,1)} %add_convert_fusion.v), custom_call_target="tpu_custom_call" | custom-call | tf_op jit(solution)/shard_map/ring_gather/pallas_call | solution.py:240
  355.1 4.6 %select_bitcast_fusion = bf16[1,1,512,2048]{3,2,1,0:T(8,128)(2,1)} fusion(bf16[1024,4096]{1,0:T(8,128)(2,1)} %ring_gather.7, s32[]{:T(128)S(6)} %select_n.73, s32[]{:T(128)S(6)} %select_n.74, bf16[1024,4096]{1,0:T(8,128)(2,1)} %ring_gather.5, pred[]{:T(512)S(6)} %eq.22), kind=kLoop, calls=%fused_computation.25 | loop fusion | flops 1048576 | bytes 6291465 | tf_op jit(solution)/shard_map/broadcast_in_dim | solution.py:379
  359.7 2.7 fusion.30.part
  362.7 15.7 %unet_tail.1 = (f32[256,16]{1,0:T(8,128)S(1)}, f32[16,512]{1,0:T(8,128)S(1)}) custom-call(f32[256,512]{1,0:T(8,128)S(1)} %fusion.30.part, bf16[256,512]{1,0:T(8,128)(2,1)S(1)} %multiply_convert_fusion.skipped, bf16[512,16]{1,0:T(8,128)(2,1)S(1)} %copy.45.w_up2, bf16[256,16]{1,0:T(8,128)(2,1)S(1)} %select_bitcast_fusion.1.weighted), custom_call_target="tpu_custom_call" | custom-call | tf_op jit(solution)/shard_map/unet_tail/pallas_call | solution.py:294
  (64 shorter events, 12.9 us)
Async XLA Ops:
  0.6 8.7 %copy-start = (bf16[512,2048]{1,0:T(8,128)(2,1)S(1)}, bf16[512,2048]{1,0:T(8,128)(2,1)}, u32[]{:S(2)}) copy-start(bf16[512,2048]{1,0:T(8,128)(2,1)} %param.22) | copy-start | bytes 6291460
  0.6 7.1 %copy-start.11 = (bf16[1,256,32]{1,2,0:T(8,128)(2,1)S(1)}, bf16[1,256,32]{1,2,0:T(8,128)(2,1)}, u32[]{:S(2)}) copy-start(bf16[1,256,32]{1,2,0:T(8,128)(2,1)} %param.14) | copy-start | bytes 49156
  0.7 6.1 %copy-start.5 = (bf16[1,64,2048]{2,1,0:T(8,128)(2,1)S(1)}, bf16[1,64,2048]{2,1,0:T(8,128)(2,1)}, u32[]{:S(2)}) copy-start(bf16[1,64,2048]{2,1,0:T(8,128)(2,1)} %param.20) | copy-start | bytes 786436
  0.7 7.1 %copy-start.10 = (bf16[32,512]{1,0:T(8,128)(2,1)S(1)}, bf16[32,512]{1,0:T(8,128)(2,1)}, u32[]{:S(2)}) copy-start(bf16[32,512]{1,0:T(8,128)(2,1)} %param.21) | copy-start | bytes 98308
  7.7 9.8 %copy-start.9 = (s32[1,512]{1,0:T(1,128)S(1)}, s32[1,512]{1,0:T(1,128)}, u32[]{:S(2)}) copy-start(s32[1,512]{1,0:T(1,128)} %param.15) | copy-start | bytes 6148
  122.9 11.7 %slice-start = ((s8[8388608]{0:T(1024)(128)(4,1)}), s8[4194304]{0:T(1024)(128)(4,1)S(1)}, s32[]{:S(2)}) async-start(s8[8388608]{0:T(1024)(128)(4,1)} %bitcast.85), calls=%async_computation | async-start | bytes 8388608
  122.9 11.7 %copy-start.6 = (f32[2,1,4096]{2,1,0:T(1,128)S(1)}, f32[2,1,4096]{2,1,0:T(1,128)}, u32[]{:S(2)}) copy-start(f32[2,1,4096]{2,1,0:T(1,128)} %get-tuple-element.11) | copy-start | bytes 98308
  122.9 11.7 %slice-start.1 = ((s8[8388608]{0:T(1024)(128)(4,1)}), s8[4194304]{0:T(1024)(128)(4,1)S(1)}, s32[]{:S(2)}) async-start(s8[8388608]{0:T(1024)(128)(4,1)} %bitcast.85), calls=%async_computation.1 | async-start | bytes 8388608
  169.1 2.4 copy-start.3
  253.2 5.8 %copy-start.2 = (bf16[1024,4096]{1,0:T(8,128)(2,1)S(1)}, bf16[1024,4096]{1,0:T(8,128)(2,1)}, u32[]{:S(2)}) copy-start(bf16[1024,4096]{1,0:T(8,128)(2,1)} %ring_gather.5) | copy-start | bytes 25165828
  276.9 2.4 copy-start.4
  355.1 7.3 %copy-start.7 = (bf16[512,16]{0,1:T(8,128)(2,1)S(1)}, bf16[512,16]{0,1:T(8,128)(2,1)}, u32[]{:S(2)}) copy-start(bf16[512,16]{0,1:T(8,128)(2,1)} %param.24) | copy-start | bytes 49156
  355.1 7.5 %copy-start.8 = (bf16[1,256,16]{1,2,0:T(8,128)(2,1)S(1)}, bf16[1,256,16]{1,2,0:T(8,128)(2,1)}, u32[]{:S(2)}) copy-start(bf16[1,256,16]{1,2,0:T(8,128)(2,1)} %param.25) | copy-start | bytes 24580
  355.1 24.6 %copy-start.1 = (bf16[512,2048]{1,0:T(8,128)(2,1)S(1)}, bf16[512,2048]{1,0:T(8,128)(2,1)}, u32[]{:S(2)}) copy-start(bf16[512,2048]{1,0:T(8,128)(2,1)} %param.22) | copy-start | bytes 6291460

commit v2 on v0

v2 whole, which is shorter than its diff:
```python
import math

import jax
import jax.numpy as jnp
from jax import lax
from jax.experimental import pallas as pl
from jax.experimental.pallas import tpu as pltpu
from jax.sharding import PartitionSpec as P

EPSILON = 1e-05
MESH = pl.DeviceIdType.MESH
ANY = pl.BlockSpec(memory_space=pl.ANY)
VM = pl.BlockSpec(memory_space=pltpu.VMEM)
RING = 4
BF16, F32 = jnp.bfloat16, jnp.float32


def dot(a, b):
    return jnp.dot(a, b, preferred_element_type=F32)


def outer(a, b):
    return lax.dot_general(a, b, (((0,), (0,)), ((), ())), preferred_element_type=F32)


class Place:
    def __init__(self):
        self.s = lax.axis_index("section")
        self.c = lax.axis_index("tp")
        d = lax.axis_index("dp")
        self.k = lax.rem(d, 2)
        self.y = lax.rem(lax.div(d, 2), RING)
        self.z = lax.div(d, 2 * RING)
        self.x = 2 * self.s + self.k

    def at(self, dx=0, dy=0, dz=0, sibling=False):
        x = lax.rem(self.x + dx, RING)
        y = lax.rem(self.y + dy, RING)
        z = lax.rem(self.z + dz, RING)
        return {
            "section": lax.div(x, 2),
            "tp": 1 - self.c if sibling else self.c,
            "dp": z * 8 + y * 2 + lax.rem(x, 2),
        }

    def partner(self):
        return {"section": self.s, "tp": self.c, "dp": self.z * 8 + self.y * 2 + 1 - self.k}


def remote(src, dst, send, recv, peer):
    return pltpu.make_async_remote_copy(
        src_ref=src, dst_ref=dst, send_sem=send, recv_sem=recv, device_id=peer, device_id_type=MESH
    )


class Spread:
    def __init__(self, me, ref, s1, r1, s2, r2):
        self.me, self.ref, self.sems = me, ref, (s1, r1, s2, r2)

    def first(self, kk, n):
        me, ref = self.me, self.ref
        s1, r1 = self.sems[:2]
        step = 1 if n % 2 == 0 else 3
        peer = me.at(dy=step) if kk == 0 else me.at(dz=step)
        if n < 2:
            part = ref.at[me.z, me.y, kk]
        else:
            back = 4 - step
            zz = me.z if kk == 0 else lax.rem(me.z + back, RING)
            yy = lax.rem(me.y + back, RING) if kk == 0 else me.y
            half = ref.shape[3] // 2
            part = ref.at[zz, yy, kk, pl.ds((n - 2) * half, half)]
        return remote(part, part, s1.at[kk, n], r1.at[kk, n], peer)

    def second(self, kk, n):
        me, ref = self.me, self.ref
        s2, r2 = self.sems[2:]
        step = 1 if n % 2 == 0 else 3
        peer = me.at(dz=step) if kk == 0 else me.at(dy=step)
        if n < 2:
            part = ref.at[me.z, :, kk] if kk == 0 else ref.at[:, me.y, kk]
        else:
            piece = pl.ds(2 * (n - 2), 2)
            back = 4 - step
            if kk == 0:
                part = ref.at[lax.rem(me.z + back, RING), piece, kk]
            else:
                part = ref.at[piece, lax.rem(me.y + back, RING), kk]
        return remote(part, part, s2.at[kk, n], r2.at[kk, n], peer)

    def own1(self):
        for kk in (0, 1):
            for n in (0, 1):
                self.first(kk, n).start()

    def pass1(self):
        for kk in (0, 1):
            for n in (0, 1):
                self.first(kk, n).wait_recv()
                self.first(kk, n + 2).start()

    def own2(self):
        for kk in (0, 1):
            for n in (2, 3):
                self.first(kk, n).wait_recv()
            for n in (0, 1):
                self.second(kk, n).start()

    def pass2(self):
        for kk in (0, 1):
            for n in (0, 1):
                self.second(kk, n).wait_recv()
                self.second(kk, n + 2).start()

    def done(self):
        for kk in (0, 1):
            for n in (2, 3):
                self.second(kk, n).wait_recv()

    def drain(self):
        for kk in (0, 1):
            for n in range(4):
                self.first(kk, n).wait_send()
                self.second(kk, n).wait_send()


class Ring:
    def __init__(self, me, ref, ss, rs):
        self.me, self.ref, self.ss, self.rs = me, ref, ss, rs

    def copy(self, n):
        me, ref = self.me, self.ref
        half = ref.shape[1] // 2

        def block(back):
            return me.c * RING + lax.rem(me.x + back, RING)

        up, down, side = me.at(dx=1), me.at(dx=3), me.at(sibling=True)
        part, peer = (
            lambda: (ref.at[block(0)], up),
            lambda: (ref.at[block(0)], down),
            lambda: (ref.at[block(0)], side),
            lambda: (ref.at[block(3), pl.ds(0, half)], up),
            lambda: (ref.at[block(1), pl.ds(half, half)], down),
            lambda: (ref.at[block(3)], side),
            lambda: (ref.at[block(1)], side),
            lambda: (ref.at[block(2)], side),
        )[n]()
        return remote(part, part, self.ss.at[n], self.rs.at[n], peer)

    def start(self):
        for n in (0, 1, 2):
            self.copy(n).start()

    def direct(self):
        self.copy(0).wait_recv()
        self.copy(3).start()
        self.copy(5).start()
        self.copy(1).wait_recv()
        self.copy(4).start()
        self.copy(6).start()

    def far(self):
        self.copy(3).wait_recv()
        self.copy(4).wait_recv()
        self.copy(7).start()

    def finish(self):
        for n in (2, 5, 6, 7):
            self.copy(n).wait_recv()

    def drain(self):
        for n in range(8):
            self.copy(n).wait_send()


def kernel(
    wq, wo_parts, wo_whole, tokens, patches, wd1, wd2, wu1, wu2, gain, meta, cot,
    hid, pred, grad,
    w_q, w_o0, w_o1, xs, heads, acc, qkv, bias, ssq, gains, metas, skip, tok, down2, up1,
    half_sum, got, upper, pair, ys, zs,
    s0q, r0q, s0o, r0o, s0w, r0w, s1, r1, s2, r2, ring_s, ring_r, sx, rx, st, rt, loc,
):
    me = Place()
    s, c, k, x, y, z = me.s, me.c, me.k, me.x, me.y, me.z
    rows = tokens.shape[0]
    img_tok = patches.shape[0]
    block = xs.shape[3]
    mine = c * RING + x
    side = me.at(sibling=True)

    loads = [
        pltpu.make_async_copy(tokens, tok, loc.at[0]),
        pltpu.make_async_copy(wd2, down2, loc.at[1]),
        pltpu.make_async_copy(wu1, up1, loc.at[2]),
        pltpu.make_async_copy(gain, gains.at[s], loc.at[3]),
        pltpu.make_async_copy(meta, metas.at[k], loc.at[4]),
    ]
    for cp in loads:
        cp.start()

    peers = ([me.at(dx=j) for j in (1, 2, 3)] + [me.at(dy=j) for j in (1, 2, 3)]
             + [me.at(dz=j) for j in (1, 2, 3)] + [side])
    barrier = pltpu.get_barrier_semaphore()
    for peer in peers:
        pl.semaphore_signal(barrier, inc=1, device_id=peer, device_id_type=MESH)
    pl.semaphore_wait(barrier, len(peers))

    def scatter_q(j):
        return remote(wq.at[lax.rem(x + j, RING)], w_q.at[s, z, y, k], s0q.at[j], r0q.at[x], me.at(dx=j))

    def scatter_o(j):
        return remote(wo_parts.at[lax.rem(x + j, RING)], w_o0.at[z, y, k], s0o.at[j], r0o.at[k],
                      me.at(dx=j))

    def whole_o():
        return remote(wo_whole, w_o1.at[z, y, k], s0w.at[0], r0w.at[k], me.partner())

    for j in (1, 2, 3):
        scatter_q(j).start()
    pltpu.make_async_copy(wq.at[x], w_q.at[s, z, y, k], r0q.at[x]).start()

    @pl.when(s == 0)
    def _():
        for j in (1, 2, 3):
            scatter_o(j).start()
        pltpu.make_async_copy(wo_parts.at[x], w_o0.at[z, y, k], r0o.at[k]).start()

    @pl.when(s == 1)
    def _():
        whole_o().start()
        pltpu.make_async_copy(wo_whole, w_o1.at[z, y, k], r0w.at[k]).start()

    for cp in loads:
        cp.wait()
    g_cp = remote(gains.at[s], gains.at[s], sx.at[3], rx.at[3], me.at(dx=2))
    m_cp = remote(metas.at[k], metas.at[k], sx.at[4], rx.at[4], me.at(dx=1))
    g_cp.start()
    m_cp.start()

    inner = dot(patches[...], wd1[...])
    skip[...] = (inner / (1.0 + jnp.exp(-inner))).astype(BF16)
    own_start, own_count = metas[k, 1:2, :], metas[k, 2:3, :]
    rr = lax.broadcasted_iota(jnp.int32, (rows, img_tok), 0)
    ii = lax.broadcasted_iota(jnp.int32, (rows, img_tok), 1)
    put = (rr == ii + own_start[:, :img_tok]).astype(F32).astype(BF16)
    rb = lax.broadcasted_iota(jnp.int32, (rows, block), 0)
    here = (rb >= own_start) & (rb < own_start + img_tok) & (own_count > 0)
    for j in range(RING):
        image = dot(skip[...], down2[:, j * block:(j + 1) * block]).astype(BF16)
        moved = dot(put, image)
        old = tok[:, j * block:(j + 1) * block].astype(F32)
        xs[k, c * RING + j] = jnp.where(here, moved, old).astype(BF16)

    own = pl.ds(c * RING, RING)
    low, high = pl.ds(0, rows // 2), pl.ds(rows // 2, rows // 2)

    def x0_copy(n):
        if n == 0:
            part, peer = xs.at[k, own, low], me.at(dx=1)
        elif n == 1:
            part, peer = xs.at[k, own, high], me.at(dx=3)
        elif n == 2:
            part, peer = xs.at[k, own], side
        elif n == 5:
            part, peer = xs.at[1 - k, own, low], side
        else:
            part, peer = xs.at[1 - k, own, high], side
        return remote(part, part, sx.at[n], rx.at[n], peer)

    for n in (0, 1, 2):
        x0_copy(n).start()

    group = [Spread(me, ref, s1.at[i], r1.at[i], s2.at[i], r2.at[i])
             for i, ref in enumerate((w_q.at[0], w_o0, w_q.at[1], w_o1))]
    q0, o0, q1, o1 = group

    def landed(ref, sem):
        pltpu.make_async_copy(ref, ref, sem).wait()

    for kk in (0, 1):
        landed(w_q.at[0, z, y, kk], r0q.at[kk])
        landed(w_o0.at[z, y, kk], r0o.at[kk])
    q0.own1()
    o0.own1()

    def mask_of(m):
        segment, start, count = metas[m, 0:1, :], metas[m, 1:2, :], metas[m, 2:3, :]
        one_hot = (lax.broadcasted_iota(jnp.int32, (8, rows), 0) == segment).astype(F32).astype(BF16)
        same = outer(one_hot, one_hot)
        i = lax.broadcasted_iota(jnp.int32, (rows, rows), 0)
        j = lax.broadcasted_iota(jnp.int32, (rows, rows), 1)
        in_i = (i >= start) & (i < start + img_tok) & (count > 0)
        in_j = (j >= start) & (j < start + img_tok)
        ok = (same > 0.5) & ((j <= i) | (in_i & in_j))
        bias[m] = jnp.where(ok, 0.0, -1e30)

    q0.pass1()
    o0.pass1()
    m_cp.wait_recv()
    g_cp.wait_recv()
    q0.own2()
    o0.own2()
    mask_of(0)
    x0_copy(0).wait_recv()
    x0_copy(5).start()
    x0_copy(1).wait_recv()
    x0_copy(6).start()
    mask_of(1)
    for n in (2, 5, 6):
        x0_copy(n).wait_recv()
    for n in (0, 1, 2, 5, 6):
        x0_copy(n).wait_send()
    q0.pass2()
    o0.pass2()
    q0.done()
    o0.done()
    for kk in (0, 1):
        landed(w_q.at[1, z, y, kk], r0q.at[2 + kk])
    q1.own1()

    def project(layer, m):
        acc[...] = jnp.zeros_like(acc)
        ssq[...] = jnp.zeros_like(ssq)

        def body(b, carry):
            values = xs[m, b].astype(F32)
            ssq[...] += jnp.sum(values * values, axis=1, keepdims=True)
            scaled = (values * gains[layer, b]).astype(BF16)
            weights = w_q[layer, lax.div(b, 2), pl.ds(2 * lax.rem(b, 2), 2)]
            acc[...] += dot(scaled, weights.reshape(block, acc.shape[1]))
            return carry

        lax.fori_loop(0, 2 * RING, body, 0)
        scale = lax.rsqrt(ssq[...] * (1.0 / (2 * RING * block)) + EPSILON)
        qkv[m] = (acc[...] * scale).astype(BF16)

    hdim = 128
    per = heads.shape[4] // hdim
    q_rows = 128

    def attend(layer, m):
        def body(i, carry):
            at = pl.ds(pl.multiple_of(i * q_rows, q_rows), q_rows)
            for h in range(per):
                base = 3 * h * hdim
                query = qkv[m, at, base:base + hdim]
                keys = qkv[m, :, base + hdim:base + 2 * hdim]
                vals = qkv[m, :, base + 2 * hdim:base + 3 * hdim]
                scores = lax.dot_general(query, keys, (((1,), (1,)), ((), ())), preferred_element_type=F32)
                scores = scores * (1.0 / math.sqrt(hdim)) + bias[m, at, :]
                probs = jnp.exp(scores - jnp.max(scores, axis=1, keepdims=True))
                probs = (probs / jnp.sum(probs, axis=1, keepdims=True)).astype(BF16)
                heads[layer, m, mine, at, h * hdim:(h + 1) * hdim] = dot(probs, vals).astype(BF16)
            return carry

        lax.fori_loop(0, rows // q_rows, body, 0)

    h_ring = [[Ring(me, heads.at[layer, m], ring_s.at[layer, m], ring_r.at[layer, m]) for m in (0, 1)]
              for layer in (0, 1)]
    x_ring = [Ring(me, xs.at[m], ring_s.at[2, m], ring_r.at[2, m]) for m in (0, 1)]

    def mix0(m):
        half_sum[...] = jnp.zeros_like(half_sum)

        def body(b, carry):
            weights = w_o0[lax.div(b, 2), pl.ds(2 * lax.rem(b, 2), 2)]
            half_sum[...] += dot(heads[0, m, b], weights.reshape(per * hdim, block))
            return carry

        lax.fori_loop(0, 2 * RING, body, 0)
        xs[m, mine] = (xs[m, mine].astype(F32) + half_sum[...]).astype(BF16)

    def section_one(act):
        pl.when(s == 1)(act)

    project(0, 0)
    q1.pass1()
    project(0, 1)
    q1.own2()
    attend(0, 0)
    h_ring[0][0].start()
    attend(0, 1)
    h_ring[0][1].start()
    h_ring[0][0].direct()
    h_ring[0][0].far()
    h_ring[0][0].finish()
    mix0(0)
    x_ring[0].start()
    q1.pass2()

    def start_o1():
        for kk in (0, 1):
            landed(w_o1.at[z, y, kk], r0w.at[kk])
        o1.own1()

    section_one(start_o1)
    h_ring[0][1].direct()
    h_ring[0][1].far()
    h_ring[0][1].finish()
    mix0(1)
    x_ring[1].start()
    section_one(o1.pass1)
    x_ring[0].direct()
    section_one(o1.own2)
    x_ring[0].far()
    x_ring[0].finish()
    q1.done()
    x_ring[1].direct()
    project(1, 0)
    attend(1, 0)
    h_ring[1][0].start()
    x_ring[1].far()
    x_ring[1].finish()
    project(1, 1)
    section_one(o1.pass2)
    attend(1, 1)
    h_ring[1][1].start()

    def put_first(j):
        return pltpu.make_async_copy(xs.at[k, c * RING + j], hid.at[:, pl.ds(j * block, block)], loc.at[j])

    @pl.when(s == 0)
    def _():
        for j in range(RING):
            put_first(j).start()

    h_ring[1][0].direct()
    h_ring[1][0].far()
    h_ring[1][1].direct()
    h_ring[1][1].far()
    h_ring[1][0].finish()
    h_ring[1][1].finish()

    def put_last(j):
        return pltpu.make_async_copy(tok.at[:, pl.ds(j * block, block)], hid.at[:, pl.ds(j * block, block)],
                                     loc.at[j])

    def tail_copy(n):
        if n == 0:
            return remote(half_sum.at[pl.ds(0, img_tok)], got, st.at[0], rt.at[0], side)
        if n == 1:
            return remote(upper, upper, st.at[1], rt.at[1], me.at(dx=2))
        if n == 2:
            return remote(pair.at[0], pair.at[1], st.at[2], rt.at[2], me.partner())
        if n < 6:
            return remote(ys.at[y], ys.at[y], st.at[n], rt.at[n], me.at(dy=n - 2))
        return remote(zs.at[z], zs.at[z], st.at[n], rt.at[n], me.at(dz=n - 5))

    @pl.when(s == 1)
    def _():
        o1.done()
        for j in range(RING):
            half_sum[...] = jnp.zeros_like(half_sum)

            def body(b, carry):
                weights = w_o1[lax.div(b, 2), pl.ds(2 * lax.rem(b, 2), 2), :, :, j * block:(j + 1) * block]
                half_sum[...] += dot(heads[1, k, b], weights.reshape(per * hdim, block))
                return carry

            lax.fori_loop(0, 2 * RING, body, 0)
            old = xs[k, c * RING + j].astype(F32)
            tok[:, j * block:(j + 1) * block] = (old + half_sum[...]).astype(BF16)
            put_last(j).start()
        ri = lax.broadcasted_iota(jnp.int32, (img_tok, rows), 0)
        ci = lax.broadcasted_iota(jnp.int32, (img_tok, rows), 1)
        take = (ci == ri + metas[k, 1:2, :]).astype(F32).astype(BF16)
        total = jnp.zeros((img_tok, up1.shape[1]), F32)
        for j in range(RING):
            final = dot(take, tok[:, j * block:(j + 1) * block]).astype(BF16)
            total = total + dot(final, up1[j * block:(j + 1) * block, :])
        half_sum[0:img_tok, :] = total
        tail_copy(0).start()
        tail_copy(0).wait_recv()
        value = half_sum[0:img_tok, :] + got[...] + skip[...].astype(F32)
        upper[...] = (value / (1.0 + jnp.exp(-value))).astype(BF16)
        tail_copy(1).start()
        tail_copy(0).wait_send()
        for j in range(RING):
            put_last(j).wait()

    @pl.when(s == 0)
    def _():
        for j in range(RING):
            put_first(j).wait()
        tail_copy(1).wait_recv()

    present = metas[k, 2:3, :wu2.shape[1]] > 0
    weighted = jnp.where(present, cot[...].astype(F32), 0.0).astype(BF16)
    pred[...] = jnp.where(present, dot(upper[...], wu2[...]), 0.0).astype(BF16)
    pair[0] = outer(weighted, upper[...])
    tail_copy(2).start()
    tail_copy(2).wait()
    ys[y] = pair[0] + pair[1]
    for n in (3, 4, 5):
        tail_copy(n).start()
    for n in (3, 4, 5):
        tail_copy(n).wait()
    zs[z] = ys[0] + ys[1] + ys[2] + ys[3]
    for n in (6, 7, 8):
        tail_copy(n).start()
    for n in (6, 7, 8):
        tail_copy(n).wait()
    grad[...] = zs[0] + zs[1] + zs[2] + zs[3]

    for j in (1, 2, 3):
        scatter_q(j).wait_send()

    @pl.when(s == 0)
    def _():
        for j in (1, 2, 3):
            scatter_o(j).wait_send()

    @pl.when(s == 1)
    def _():
        whole_o().wait_send()
        o1.drain()
        tail_copy(1).wait_send()

    g_cp.wait_send()
    m_cp.wait_send()
    for g in (q0, o0, q1):
        g.drain()
    for r in h_ring[0] + h_ring[1] + x_ring:
        r.drain()


def window(wq, wo_parts, wo_whole, tokens, patches, wd1, wd2, wu1, wu2, gain, meta, cot):
    rows, width = tokens.shape
    block = width // RING
    depth, wide_q = wq.shape[1:]
    depth_o = wo_whole.shape[0]
    img_tok = patches.shape[0]
    channels = wd1.shape[1]
    pix = wu2.shape[1]
    head_cols = wide_q // 3
    dma = pltpu.SemaphoreType.DMA
    vm = pltpu.VMEM
    scratch = [
        vm((2, RING, RING, 2, depth, wide_q), BF16),
        vm((RING, RING, 2, depth_o, block), BF16),
        vm((RING, RING, 2, depth_o, width), BF16),
        vm((2, 2 * RING, rows, block), BF16),
        vm((2, 2, 2 * RING, rows, head_cols), BF16),
        vm((rows, wide_q), F32),
        vm((2, rows, wide_q), BF16),
        vm((2, rows, rows), F32),
        vm((rows, 1), F32),
        vm((2,) + gain.shape, F32),
        vm((2,) + meta.shape, jnp.int32),
        vm((img_tok, channels), BF16),
        vm((rows, width), BF16),
        vm(wd2.shape, BF16),
        vm(wu1.shape, BF16),
        vm((rows, block), F32),
        vm((img_tok, channels), F32),
        vm((img_tok, channels), BF16),
        vm((2, pix, channels), F32),
        vm((RING, pix, channels), F32),
        vm((RING, pix, channels), F32),
        dma((4,)), dma((4,)), dma((4,)), dma((2,)), dma((1,)), dma((2,)),
        dma((4, 2, 4)), dma((4, 2, 4)), dma((4, 2, 4)), dma((4, 2, 4)),
        dma((3, 2, 8)), dma((3, 2, 8)), dma((7,)), dma((7,)), dma((9,)), dma((9,)), dma((5,)),
    ]
    return pl.pallas_call(
        kernel,
        out_shape=(
            jax.ShapeDtypeStruct((rows, width), BF16),
            jax.ShapeDtypeStruct((img_tok, pix), BF16),
            jax.ShapeDtypeStruct((pix, channels), F32),
        ),
        in_specs=[ANY, ANY, ANY, ANY, VM, VM, ANY, ANY, VM, ANY, ANY, VM],
        out_specs=(ANY, VM, VM),
        scratch_shapes=scratch,
        compiler_params=pltpu.CompilerParams(collective_id=0, has_side_effects=True,
                                             vmem_limit_bytes=63 << 20),
        name="window",
    )(wq, wo_parts, wo_whole, tokens, patches, wd1, wd2, wu1, wu2, gain, meta, cot)


def shards(
    tokens_in, patches, segment_ids, img_start, img_count, norm_gain, w_qkv, w_out, w_down1, w_down2,
    w_up1, w_up2, cotangent,
):
    rows, width = tokens_in.shape[1:]
    depth, heads, three, hdim = w_qkv.shape[1:]
    wide_q = heads // RING * three * hdim
    block = width // RING
    wq = jnp.transpose(w_qkv[0].reshape(depth, RING, wide_q), (1, 0, 2))
    wo = jnp.transpose(w_out[0].reshape(w_out.shape[1], RING, block), (1, 0, 2))
    meta = jnp.concatenate(
        [segment_ids, jnp.broadcast_to(img_start[:, None], (1, rows)),
         jnp.broadcast_to(img_count[:, None], (1, rows)), jnp.zeros((5, rows), jnp.int32)], axis=0)
    gain = norm_gain.reshape(2 * RING, 1, block)
    hidden, pred, grad = window(wq, wo, w_out[0], tokens_in[0], patches[0], w_down1, w_down2, w_up1,
                                w_up2, gain, meta, cotangent[0])
    return (hidden[None, None], pred[None], grad.T)


def solution(mesh):
    placed = (
        P("dp", None, "tp"),
        P("dp", None, None),
        P("dp", None),
        P("dp"),
        P("dp"),
        P("section", None),
        P("section", "dp", "tp", None, None),
        P("section", "dp", "tp"),
        P(),
        P(None, "tp"),
        P("tp", None),
        P(None, "section"),
        P("dp", None, "section"),
    )
    return jax.shard_map(
        shards,
        mesh=mesh,
        in_specs=placed,
        out_specs=(P("section", "dp", None, "tp"), P("dp", None, "section"), P(None, "section")),
        check_vma=False,
    )
```

time: 1290 us -> 228 us (0.18)
  waiting for transfers between devices: 973 us -> 0 us
  Pallas kernels: 0 us -> 209 us
  blocking collectives: 158 us -> 0 us
  matrix products: 63.7 us -> 0 us
  other arithmetic: 29.3 us -> 1.36 us
  starting transfers between devices: 22.1 us -> 0 us
  between operations: 15.5 us -> 1.95 us
    all_gather x6 -> x0, waiting for transfers between devices: 825 us -> none  [the longest x1 537 us: shards(): lax.all_gather(w_qkv, 'dp', axis=1, tiled=True)]
    pallas_call x0 -> x1, Pallas kernels: none -> 209 us  [window(): pl.pallas_call(kernel, out_shape=(jax.ShapeDtypeStruct((rows, width), BF1...]
    psum x1 -> x0, blocking collectives: 158 us -> none  [shards(): lax.psum(grad_local.astype(jnp.bfloat16), 'dp').astype(jnp.float32)]
    ppermute x4 -> x0, waiting for transfers between devices: 88.3 us -> none  [passed_along(): return lax.ppermute(value, axis, pairs)]
    dot_general x23 -> x0, matrix products: 63.7 us -> none  [the longest x1 19.1 us: attend(): jnp.einsum('rd,dhtk->htrk', normed, weights_qkv, preferred_element_type=j...]
    psum x2 -> x0, waiting for transfers between devices: 59.9 us -> none  [the longest x1 33.4 us: broadcast(): return lax.psum(block, axis)]
    ppermute x4 -> x0, starting transfers between devices: 21.9 us -> none  [passed_along(): return lax.ppermute(value, axis, pairs)]
  transfers between devices with their start and end apart: 12 -> 0, of which waited for: 10 -> 0; matrix products, arithmetic and copies ran while one was open for 2% -> 0% of each run, Pallas kernels for 0% -> 0%
where the time goes in v2:
time: 228 us; the launch traced here: 227 us
  Pallas kernels  209 us (92%)
  local copies, waits for them, and re-layouts  14.5 us (6%)
    pallas_call x1, Pallas kernels, window(): pl.pallas_call(kernel, out_shape=(jax.ShapeDtypeStruct((rows, width), BF1...  209 us
    unnamed x9, local copies, waits for them, and re-layouts  11.2 us

profile of v2, /device:TPU:0, one launch (start us, length us, event | category | flops | bytes accessed | tf_op | source)
XLA Modules:
  0.0 227.1 jit_solution(8230998893224378042)
XLA Ops:
  1.9 0.1 pad.1.clone
  2.0 0.1 pad.2.clone
  2.1 0.1 pad.3.clone
  2.1 1.4 add_add_fusion.meta
  3.5 1.4 copy.23
  5.0 1.4 copy.24
  6.4 1.5 copy.25.wu2
  7.8 1.1 reshape_squeeze.7
  9.0 0.8 copy.28
  9.8 1.6 copy.20
  11.4 1.2 copy.21
  12.5 209.2 %window.1 = (bf16[512,2048]{1,0:T(8,128)(2,1)}, bf16[256,16]{1,0:T(8,128)(2,1)}, f32[16,512]{1,0:T(8,128)}) custom-call(bf16[4,128,768]{2,1,0:T(8,128)(2,1)} %bitcast.16, bf16[4,64,512]{2,1,0:T(8,128)(2,1)} %bitcast.20, bf16[64,2048]{1,0:T(8,128)(2,1)} %bitcast.19, bf16[512,2048]{1,0:T(8,128)(2,1)} %bitcast.18, bf16[256,32]{1,0:T(8,128)(2,1)} %bitcast.21, ...), custom_call_target="tpu_custom_call" | custom-call | tf_op jit(solution)/shard_map/window/pallas_call | solution.py:565
  221.8 1.5 copy.26
  223.3 0.0 copy-start
  223.3 3.2 %copy.33 = bf16[1,1,512,2048]{3,2,1,0:T(8,128)(2,1)} copy(bf16[1,1,512,2048]{3,2,1,0:T(8,128)(2,1)} %bitcast.17) | data formatting | bytes 4194304
  226.5 0.0 copy-done
  226.5 0.6 copy.34
  (1 shorter events, 0.0 us)
Async XLA Ops:
  223.3 3.2 %copy-start = (f32[16,512]{1,0:T(8,128)S(1)}, f32[16,512]{1,0:T(8,128)}, u32[]{:S(2)}) copy-start(f32[16,512]{1,0:T(8,128)} %get-tuple-element.8) | copy-start | bytes 98308

commit v3 on v2

v3 whole, which is shorter than its diff:
```python
import math

import jax
import jax.numpy as jnp
from jax import lax
from jax.experimental import pallas as pl
from jax.experimental.pallas import tpu as pltpu
from jax.sharding import PartitionSpec as P

EPSILON = 1e-05
MESH = pl.DeviceIdType.MESH
ANY = pl.BlockSpec(memory_space=pl.ANY)
VM = pl.BlockSpec(memory_space=pltpu.VMEM)
RING = 4
BF16, F32 = jnp.bfloat16, jnp.float32


def dot(a, b):
    return jnp.dot(a, b, preferred_element_type=F32)


def outer(a, b):
    return lax.dot_general(a, b, (((0,), (0,)), ((), ())), preferred_element_type=F32)


class Place:
    def __init__(self):
        self.s = lax.axis_index("section")
        self.c = lax.axis_index("tp")
        d = lax.axis_index("dp")
        self.k = lax.rem(d, 2)
        self.y = lax.rem(lax.div(d, 2), RING)
        self.z = lax.div(d, 2 * RING)
        self.x = 2 * self.s + self.k

    def at(self, dx=0, dy=0, dz=0, sibling=False):
        x = lax.rem(self.x + dx, RING)
        y = lax.rem(self.y + dy, RING)
        z = lax.rem(self.z + dz, RING)
        return {
            "section": lax.div(x, 2),
            "tp": 1 - self.c if sibling else self.c,
            "dp": z * 8 + y * 2 + lax.rem(x, 2),
        }

    def partner(self):
        return {"section": self.s, "tp": self.c, "dp": self.z * 8 + self.y * 2 + 1 - self.k}


def remote(src, dst, send, recv, peer):
    return pltpu.make_async_remote_copy(
        src_ref=src, dst_ref=dst, send_sem=send, recv_sem=recv, device_id=peer, device_id_type=MESH
    )


class Spread:
    def __init__(self, me, ref, s1, r1, s2, r2):
        self.me, self.ref, self.sems = me, ref, (s1, r1, s2, r2)

    def first(self, kk, n):
        me, ref = self.me, self.ref
        s1, r1 = self.sems[:2]
        step = 1 if n % 2 == 0 else 3
        peer = me.at(dy=step) if kk == 0 else me.at(dz=step)
        if n < 2:
            part = ref.at[me.z, me.y, kk]
        else:
            back = 4 - step
            zz = me.z if kk == 0 else lax.rem(me.z + back, RING)
            yy = lax.rem(me.y + back, RING) if kk == 0 else me.y
            half = ref.shape[3] // 2
            part = ref.at[zz, yy, kk, pl.ds((n - 2) * half, half)]
        return remote(part, part, s1.at[kk, n], r1.at[kk, n], peer)

    def second(self, kk, n):
        me, ref = self.me, self.ref
        s2, r2 = self.sems[2:]
        step = 1 if n % 2 == 0 else 3
        peer = me.at(dz=step) if kk == 0 else me.at(dy=step)
        if n < 2:
            part = ref.at[me.z, :, kk] if kk == 0 else ref.at[:, me.y, kk]
        else:
            piece = pl.ds(2 * (n - 2), 2)
            back = 4 - step
            if kk == 0:
                part = ref.at[lax.rem(me.z + back, RING), piece, kk]
            else:
                part = ref.at[piece, lax.rem(me.y + back, RING), kk]
        return remote(part, part, s2.at[kk, n], r2.at[kk, n], peer)

    def own1(self):
        for kk in (0, 1):
            for n in (0, 1):
                self.first(kk, n).start()

    def pass1(self):
        for kk in (0, 1):
            for n in (0, 1):
                self.first(kk, n).wait_recv()
                self.first(kk, n + 2).start()

    def own2(self):
        for kk in (0, 1):
            for n in (2, 3):
                self.first(kk, n).wait_recv()
            for n in (0, 1):
                self.second(kk, n).start()

    def pass2(self):
        for kk in (0, 1):
            for n in (0, 1):
                self.second(kk, n).wait_recv()
                self.second(kk, n + 2).start()

    def done(self):
        for kk in (0, 1):
            for n in (2, 3):
                self.second(kk, n).wait_recv()

    def drain(self):
        for kk in (0, 1):
            for n in range(4):
                self.first(kk, n).wait_send()
                self.second(kk, n).wait_send()


class Ring:
    def __init__(self, me, ref, ss, rs):
        self.me, self.ref, self.ss, self.rs = me, ref, ss, rs

    def copy(self, n):
        me, ref = self.me, self.ref
        half = ref.shape[1] // 2

        def block(back):
            return me.c * RING + lax.rem(me.x + back, RING)

        up, down, side = me.at(dx=1), me.at(dx=3), me.at(sibling=True)
        part, peer = (
            lambda: (ref.at[block(0)], up),
            lambda: (ref.at[block(0)], down),
            lambda: (ref.at[block(0)], side),
            lambda: (ref.at[block(3), pl.ds(0, half)], up),
            lambda: (ref.at[block(1), pl.ds(half, half)], down),
            lambda: (ref.at[block(3)], side),
            lambda: (ref.at[block(1)], side),
            lambda: (ref.at[block(2)], side),
        )[n]()
        return remote(part, part, self.ss.at[n], self.rs.at[n], peer)

    def start(self):
        for n in (0, 1, 2):
            self.copy(n).start()

    def direct(self):
        self.copy(0).wait_recv()
        self.copy(3).start()
        self.copy(5).start()
        self.copy(1).wait_recv()
        self.copy(4).start()
        self.copy(6).start()

    def far(self):
        self.copy(3).wait_recv()
        self.copy(4).wait_recv()
        self.copy(7).start()

    def finish(self):
        for n in (2, 5, 6, 7):
            self.copy(n).wait_recv()

    def drain(self):
        for n in range(8):
            self.copy(n).wait_send()


def kernel(
    wq, wo, tokens, patches_t, wd1, wd2, wu1, wu2_t, gain, segment, start_in, count_in, cot_t,
    hid, pred, grad,
    w_q, w_o0, w_o1, xs, heads, acc, qkv, bias, ssq, gains, metas, skip, down2, up1,
    part, got, upper, cots, ups, p_own, p_in, g_own, g_in, pair, ys, zs,
    s0q, r0q, s0o, r0o, s0w, r0w, s1, r1, s2, r2, ring_s, ring_r, sx, rx, st, rt, loc,
):
    me = Place()
    s, c, k, x, y, z = me.s, me.c, me.k, me.x, me.y, me.z
    rows = tokens.shape[0]
    img_tok = patches_t.shape[1]
    block = xs.shape[3]
    mine = c * RING + x
    side = me.at(sibling=True)

    loads = [
        pltpu.make_async_copy(tokens, hid, loc.at[0]),
        pltpu.make_async_copy(wd2, down2, loc.at[1]),
        pltpu.make_async_copy(wu1, up1, loc.at[2]),
        pltpu.make_async_copy(gain, gains.at[s], loc.at[3]),
    ]
    for cp in loads:
        cp.start()
    metas[k, 0:1, :] = segment[...]
    metas[k, 1:2, :] = jnp.full((1, rows), start_in[0], jnp.int32)
    metas[k, 2:3, :] = jnp.full((1, rows), count_in[0], jnp.int32)
    metas[k, 3:8, :] = jnp.zeros((5, rows), jnp.int32)

    peers = ([me.at(dx=j) for j in (1, 2, 3)] + [me.at(dy=j) for j in (1, 2, 3)]
             + [me.at(dz=j) for j in (1, 2, 3)] + [side])
    across = dict(me.at(dx=2), tp=1 - c)
    barrier = pltpu.get_barrier_semaphore()
    for peer in peers + [across]:
        pl.semaphore_signal(barrier, inc=1, device_id=peer, device_id_type=MESH)
    pl.semaphore_wait(barrier, len(peers) + 1)

    def scatter_q(j):
        return remote(wq.at[lax.rem(x + j, RING)], w_q.at[s, z, y, k], s0q.at[j], r0q.at[x], me.at(dx=j))

    def scatter_o(j):
        cols = pl.ds(pl.multiple_of(lax.rem(x + j, RING) * block, block), block)
        return remote(wo.at[:, cols], w_o0.at[z, y, k], s0o.at[j], r0o.at[k], me.at(dx=j))

    def whole_o():
        return remote(wo, w_o1.at[z, y, k], s0w.at[0], r0w.at[k], me.partner())

    def start_q():
        for j in (1, 3, 2):
            scatter_q(j).start()
        pltpu.make_async_copy(wq.at[x], w_q.at[s, z, y, k], r0q.at[x]).start()

    def start_o():
        for j in (1, 3, 2):
            scatter_o(j).start()
        own_cols = pl.ds(pl.multiple_of(x * block, block), block)
        pltpu.make_async_copy(wo.at[:, own_cols], w_o0.at[z, y, k], r0o.at[k]).start()

    def start_w():
        whole_o().start()
        pltpu.make_async_copy(wo, w_o1.at[z, y, k], r0w.at[k]).start()

    section_zero, section_one = pl.when(s == 0), pl.when(s == 1)
    section_zero(start_q)

    for cp in loads:
        cp.wait()
    g_cp = remote(gains.at[s], gains.at[s], sx.at[3], rx.at[3], me.at(dx=2))
    m_cp = remote(metas.at[k], metas.at[k], sx.at[4], rx.at[4], me.at(dx=1))
    g_cp.start()
    m_cp.start()

    def give(n):
        src, dst = ((cot_t, cots), (wu2_t, ups))[n - 7]
        return remote(src, dst, sx.at[n], rx.at[n], me.at(dx=2))

    @pl.when((s == 0) & (c == 0))
    def _():
        give(7).start()
        give(8).start()

    @pl.when((s == 1) & (c == 1))
    def _():
        cots[...] = cot_t[...]
        ups[...] = wu2_t[...]

    inner = outer(patches_t[...], wd1[...])
    skip[...] = (inner / (1.0 + jnp.exp(-inner))).astype(BF16)
    own_start, own_count = metas[k, 1:2, :], metas[k, 2:3, :]
    rr = lax.broadcasted_iota(jnp.int32, (rows, img_tok), 0)
    ii = lax.broadcasted_iota(jnp.int32, (rows, img_tok), 1)
    put = (rr == ii + own_start[:, :img_tok]).astype(F32).astype(BF16)
    rb = lax.broadcasted_iota(jnp.int32, (rows, block), 0)
    here = (rb >= own_start) & (rb < own_start + img_tok) & (own_count > 0)
    for j in range(RING):
        image = dot(skip[...], down2[:, j * block:(j + 1) * block]).astype(BF16)
        moved = dot(put, image)
        old = hid[:, j * block:(j + 1) * block].astype(F32)
        xs[k, c * RING + j] = jnp.where(here, moved, old).astype(BF16)

    own = pl.ds(c * RING, RING)
    low, high = pl.ds(0, rows // 2), pl.ds(rows // 2, rows // 2)

    def x0_copy(n):
        if n == 0:
            what, peer = xs.at[k, own, low], me.at(dx=1)
        elif n == 1:
            what, peer = xs.at[k, own, high], me.at(dx=3)
        elif n == 2:
            what, peer = xs.at[k, own], side
        elif n == 5:
            what, peer = xs.at[1 - k, own, low], side
        else:
            what, peer = xs.at[1 - k, own, high], side
        return remote(what, what, sx.at[n], rx.at[n], peer)

    group = [Spread(me, ref, s1.at[i], r1.at[i], s2.at[i], r2.at[i])
             for i, ref in enumerate((w_q.at[0], w_o0, w_q.at[1], w_o1))]
    q0, o0, q1, o1 = group

    def landed(ref, sem):
        pltpu.make_async_copy(ref, ref, sem).wait()

    def mask_of(m):
        segment, start, count = metas[m, 0:1, :], metas[m, 1:2, :], metas[m, 2:3, :]
        one_hot = (lax.broadcasted_iota(jnp.int32, (8, rows), 0) == segment).astype(F32).astype(BF16)
        same = outer(one_hot, one_hot)
        i = lax.broadcasted_iota(jnp.int32, (rows, rows), 0)
        j = lax.broadcasted_iota(jnp.int32, (rows, rows), 1)
        in_i = (i >= start) & (i < start + img_tok) & (count > 0)
        in_j = (j >= start) & (j < start + img_tok)
        ok = (same > 0.5) & ((j <= i) | (in_i & in_j))
        bias[m] = jnp.where(ok, 0.0, -1e30)

    for kk in (0, 1):
        landed(w_q.at[0, z, y, kk], r0q.at[kk])
    q0.own1()
    for n in (0, 1, 2):
        x0_copy(n).start()
    section_zero(start_o)
    q0.pass1()
    m_cp.wait_recv()
    g_cp.wait_recv()
    mask_of(0)
    q0.own2()
    mask_of(1)
    x0_copy(0).wait_recv()
    x0_copy(5).start()
    x0_copy(1).wait_recv()
    x0_copy(6).start()

    @section_one
    def _():
        start_q()
        start_w()

    q0.pass2()
    for kk in (0, 1):
        landed(w_o0.at[z, y, kk], r0o.at[kk])
    o0.own1()
    for n in (2, 5, 6):
        x0_copy(n).wait_recv()

    def band(m, step, first=False):
        pieces, squares = [], 0.0
        zz, yy = lax.rem(z + step, RING), lax.rem(y + step, RING)

        def take(b, at):
            values = xs[m, b, :, at].astype(F32)
            pieces.append((values * gains[0, b, :, at]).astype(BF16))
            return jnp.sum(values * values, axis=1, keepdims=True)

        half = block // 2
        depth = half // 2
        for b in (0, 1):
            for at in (0, half):
                squares += take(2 * zz + b, slice(at, at + depth))
        for b in range(RING):
            at = pl.ds(pl.multiple_of(lax.rem(yy, 2) * half + depth, depth), depth)
            squares += take(2 * b + lax.div(yy, 2), at)
        weights = jnp.concatenate(
            [w_q[0, zz, :, 0].reshape(block, acc.shape[2]), w_q[0, :, yy, 1].reshape(block, acc.shape[2])], axis=0)
        total = dot(jnp.concatenate(pieces, axis=1), weights)
        if first:
            acc[m] = total
            ssq[m] = squares
        else:
            acc[m] += total
            ssq[m] += squares

    def scaled(m):
        scale = lax.rsqrt(ssq[m] * (1.0 / (2 * RING * block)) + EPSILON)
        qkv[m] = (acc[m] * scale).astype(BF16)

    def project1(m):
        ssq[m] = jnp.zeros_like(ssq[m])
        for b in range(0, 2 * RING, 2):
            pieces = []
            for n in (b, b + 1):
                values = xs[m, n].astype(F32)
                ssq[m] += jnp.sum(values * values, axis=1, keepdims=True)
                pieces.append((values * gains[1, n]).astype(BF16))
            total = dot(jnp.concatenate(pieces, axis=1), w_q[1, b // 2].reshape(2 * block, acc.shape[2]))
            if b == 0:
                acc[m] = total
            else:
                acc[m] += total
        scaled(m)

    hdim = 128
    per = heads.shape[3] // hdim
    q_rows = 128

    def attend(layer, m):
        for i in range(rows // q_rows):
            at = pl.ds(i * q_rows, q_rows)
            for h in range(per):
                base = 3 * h * hdim
                query = qkv[m, at, base:base + hdim]
                keys = qkv[m, :, base + hdim:base + 2 * hdim]
                vals = qkv[m, :, base + 2 * hdim:base + 3 * hdim]
                scores = lax.dot_general(query, keys, (((1,), (1,)), ((), ())), preferred_element_type=F32)
                scores = scores * (1.0 / math.sqrt(hdim)) + bias[m, at, :]
                probs = jnp.exp(scores - jnp.max(scores, axis=1, keepdims=True))
                probs = (probs * (1.0 / jnp.sum(probs, axis=1, keepdims=True))).astype(BF16)
                heads[m, mine, at, h * hdim:(h + 1) * hdim] = dot(probs, vals).astype(BF16)

    h_ring = [[Ring(me, heads.at[m], ring_s.at[layer, m], ring_r.at[layer, m]) for m in (0, 1)]
              for layer in (0, 1)]
    x_ring = [Ring(me, xs.at[m], ring_s.at[2, m], ring_r.at[2, m]) for m in (0, 1)]

    def mix0(m):
        together = jnp.concatenate([heads[m, b] for b in range(2 * RING)], axis=1)
        added = dot(together, w_o0[...].reshape(2 * RING * per * hdim, block))
        xs[m, mine] = (xs[m, mine].astype(F32) + added).astype(BF16)

    for step in (0, 1, 3):
        for m in (0, 1):
            band(m, step, step == 0)
    for n in (0, 1, 2, 5, 6):
        x0_copy(n).wait_send()
    q0.done()
    o0.pass1()
    band(0, 2)
    scaled(0)
    attend(0, 0)
    h_ring[0][0].start()
    o0.own2()
    band(1, 2)
    scaled(1)
    attend(0, 1)
    h_ring[0][1].start()
    o0.pass2()
    for kk in (0, 1):
        landed(w_q.at[1, z, y, kk], r0q.at[2 + kk])
    q1.own1()
    h_ring[0][0].direct()
    h_ring[0][0].far()
    h_ring[0][0].finish()
    o0.done()
    mix0(0)
    h_ring[0][0].drain()
    x_ring[0].start()
    q1.pass1()
    h_ring[0][1].direct()
    h_ring[0][1].far()
    h_ring[0][1].finish()
    mix0(1)
    h_ring[0][1].drain()
    x_ring[1].start()
    q1.own2()

    @section_one
    def _():
        for kk in (0, 1):
            landed(w_o1.at[z, y, kk], r0w.at[kk])
        o1.own1()

    x_ring[0].direct()
    x_ring[0].far()
    section_one(o1.pass1)
    q1.pass2()
    section_one(o1.own2)
    x_ring[0].finish()
    x_ring[1].direct()
    q1.done()
    project1(0)
    attend(1, 0)
    h_ring[1][0].start()
    x_ring[1].far()
    section_one(o1.pass2)
    x_ring[1].finish()
    project1(1)
    h_ring[1][0].direct()
    attend(1, 1)
    h_ring[1][1].start()

    @section_zero
    def _():
        for j in range(RING):
            hid[:, j * block:(j + 1) * block] = xs[k, c * RING + j]

    h_ring[1][0].far()
    h_ring[1][1].direct()
    h_ring[1][1].far()
    h_ring[1][0].finish()
    h_ring[1][1].finish()

    def tail_copy(n):
        if n == 0:
            return remote(part, got, st.at[0], rt.at[0], side)
        if n == 2:
            return remote(pair.at[0], pair.at[1], st.at[2], rt.at[2], me.partner())
        if n < 6:
            return remote(ys.at[y], ys.at[y], st.at[n], rt.at[n], me.at(dy=n - 2))
        return remote(zs.at[z], zs.at[z], st.at[n], rt.at[n], me.at(dz=n - 5))

    def result_copy(n, core):
        src, dst = ((p_own, p_in), (g_own, g_in))[n]
        peer = side if core is None else dict(me.at(dx=2), tp=core)
        index = 0 if core is None else core
        return remote(src, dst, st.at[9 + 2 * n + index], rt.at[9 + n], peer)

    def send_result(n):
        @pl.when(c == 0)
        def _():
            result_copy(n, 0).start()
            result_copy(n, 1).start()

        @pl.when(c == 1)
        def _():
            result_copy(n, None).start()

    @section_one
    def _():
        @pl.when(c == 0)
        def _():
            give(7).wait_recv()
            give(8).wait_recv()

        o1.done()
        together = jnp.concatenate([heads[k, b] for b in range(2 * RING)], axis=1)
        for j in range(RING):
            at = slice(j * block, (j + 1) * block)
            added = dot(together, w_o1[:, :, :, :, at].reshape(2 * RING * per * hdim, block))
            hid[:, at] = (xs[k, c * RING + j].astype(F32) + added).astype(BF16)
        ri = lax.broadcasted_iota(jnp.int32, (img_tok, rows), 0)
        ci = lax.broadcasted_iota(jnp.int32, (img_tok, rows), 1)
        take = (ci == ri + metas[k, 1:2, :]).astype(F32).astype(BF16)
        total = jnp.zeros(part.shape, F32)
        for j in range(RING):
            at = slice(j * block, (j + 1) * block)
            total = total + dot(dot(take, hid[:, at]).astype(BF16), up1[at, :])
        part[...] = total
        tail_copy(0).start()
        tail_copy(0).wait_recv()
        value = part[...] + got[...] + skip[...].astype(F32)
        upper[...] = (value / (1.0 + jnp.exp(-value))).astype(BF16)
        present = metas[k, 2:3, :img_tok] > 0
        weighted = jnp.where(present, cots[...].astype(F32), 0.0).astype(BF16)
        pair[0] = dot(weighted, upper[...])
        tail_copy(2).start()
        guess = lax.dot_general(ups[...], upper[...], (((1,), (1,)), ((), ())), preferred_element_type=F32)
        p_own[...] = jnp.where(present, guess, 0.0).astype(BF16)
        send_result(0)
        tail_copy(2).wait()
        ys[y] = pair[0] + pair[1]
        for n in (3, 4, 5):
            tail_copy(n).start()
        for n in (3, 4, 5):
            tail_copy(n).wait()
        zs[z] = ys[0] + ys[1] + ys[2] + ys[3]
        for n in (6, 7, 8):
            tail_copy(n).start()
        for n in (6, 7, 8):
            tail_copy(n).wait()
        g_own[...] = zs[0] + zs[1] + zs[2] + zs[3]
        send_result(1)
        tail_copy(0).wait_send()

    for j in (1, 2, 3):
        scatter_q(j).wait_send()

    @section_zero
    def _():
        for j in (1, 2, 3):
            scatter_o(j).wait_send()

        @pl.when(c == 0)
        def _():
            give(7).wait_send()
            give(8).wait_send()

    @section_one
    def _():
        whole_o().wait_send()
        o1.drain()

    g_cp.wait_send()
    m_cp.wait_send()
    for g in (q0, o0, q1):
        g.drain()
    for r in h_ring[1] + x_ring:
        r.drain()

    @pl.when((s == 1) & (c == 1))
    def _():
        pred[...] = p_own[...]
        grad[...] = g_own[...]
        result_copy(0, None).wait_send()
        result_copy(1, None).wait_send()

    @pl.when((s == 0) | (c == 0))
    def _():
        result_copy(0, None).wait_recv()
        result_copy(1, None).wait_recv()
        pred[...] = p_in[...]
        grad[...] = g_in[...]

    @pl.when((s == 1) & (c == 0))
    def _():
        for n in (0, 1):
            for core in (0, 1):
                result_copy(n, core).wait_send()


def window(wq, wo, tokens, patches_t, wd1, wd2, wu1, wu2_t, gain, segment, start, count, cot_t):
    rows, width = tokens.shape
    block = width // RING
    depth, wide_q = wq.shape[1:]
    depth_o = wo.shape[0]
    img_tok = patches_t.shape[1]
    channels = wd1.shape[1]
    pix = wu2_t.shape[0]
    head_cols = wide_q // 3
    dma = pltpu.SemaphoreType.DMA
    vm = pltpu.VMEM
    scratch = [
        vm((2, RING, RING, 2, depth, wide_q), BF16),
        vm((RING, RING, 2, depth_o, block), BF16),
        vm((RING, RING, 2, depth_o, width), BF16),
        vm((2, 2 * RING, rows, block), BF16),
        vm((2, 2 * RING, rows, head_cols), BF16),
        vm((2, rows, wide_q), F32),
        vm((2, rows, wide_q), BF16),
        vm((2, rows, rows), F32),
        vm((2, rows, 1), F32),
        vm((2,) + gain.shape, F32),
        vm((2, 8, rows), jnp.int32),
        vm((img_tok, channels), BF16),
        vm(wd2.shape, BF16),
        vm(wu1.shape, BF16),
        vm((img_tok, channels), F32),
        vm((img_tok, channels), F32),
        vm((img_tok, channels), BF16),
        vm(cot_t.shape, BF16),
        vm(wu2_t.shape, BF16),
        vm((pix, img_tok), BF16),
        vm((pix, img_tok), BF16),
        vm((pix, channels), F32),
        vm((pix, channels), F32),
        vm((2, pix, channels), F32),
        vm((RING, pix, channels), F32),
        vm((RING, pix, channels), F32),
        dma((4,)), dma((4,)), dma((4,)), dma((2,)), dma((1,)), dma((2,)),
        dma((4, 2, 4)), dma((4, 2, 4)), dma((4, 2, 4)), dma((4, 2, 4)),
        dma((3, 2, 8)), dma((3, 2, 8)), dma((9,)), dma((9,)), dma((13,)), dma((11,)), dma((4,)),
    ]
    sm = pl.BlockSpec(memory_space=pltpu.SMEM)
    return pl.pallas_call(
        kernel,
        out_shape=(
            jax.ShapeDtypeStruct((rows, width), BF16),
            jax.ShapeDtypeStruct((pix, img_tok), BF16),
            jax.ShapeDtypeStruct((pix, channels), F32),
        ),
        in_specs=[ANY, ANY, ANY, VM, VM, ANY, ANY, VM, ANY, VM, sm, sm, VM],
        out_specs=(VM, VM, VM),
        scratch_shapes=scratch,
        compiler_params=pltpu.CompilerParams(collective_id=0, has_side_effects=True,
                                             vmem_limit_bytes=63 << 20),
        name="window",
    )(wq, wo, tokens, patches_t, wd1, wd2, wu1, wu2_t, gain, segment, start, count, cot_t)


def shards(
    tokens_in, patches, segment_ids, img_start, img_count, norm_gain, w_qkv, w_out, w_down1, w_down2,
    w_up1, w_up2, cotangent,
):
    rows, width = tokens_in.shape[1:]
    depth, heads, three, hdim = w_qkv.shape[1:]
    wide_q = heads // RING * three * hdim
    block = width // RING
    wq = jnp.transpose(w_qkv[0].reshape(depth, RING, wide_q), (1, 0, 2))
    gain = norm_gain.reshape(2 * RING, 1, block)
    hidden, pred, grad = window(wq, w_out[0], tokens_in[0], patches[0].T, w_down1, w_down2, w_up1,
                                w_up2.T, gain, segment_ids, img_start, img_count, cotangent[0].T)
    return (hidden[None, None], pred.T[None], grad.T)


def solution(mesh):
    placed = (
        P("dp", None, "tp"),
        P("dp", None, None),
        P("dp", None),
        P("dp"),
        P("dp"),
        P("section", None),
        P("section", "dp", "tp", None, None),
        P("section", "dp", "tp"),
        P(),
        P(None, "tp"),
        P("tp", None),
        P(None, "section"),
        P("dp", None, "section"),
    )
    return jax.shard_map(
        shards,
        mesh=mesh,
        in_specs=placed,
        out_specs=(P("section", "dp", None, "tp"), P("dp", None, "section"), P(None, "section")),
        check_vma=False,
    )
```

time: 228 us -> 214 us (0.939)
  local copies, waits for them, and re-layouts: 14.5 us -> 7.16 us
  Pallas kernels: 209 us -> 203 us
    pallas_call x1, Pallas kernels: 209 us -> 203 us  [window(): pl.pallas_call(kernel, out_shape=(jax.ShapeDtypeStruct((rows, width), BF1...]
    unnamed x9 -> x8, local copies, waits for them, and re-layouts: 11.2 us -> 6 us
where the time goes in v3:
time: 214 us; the launch traced here: 213 us
  Pallas kernels  203 us (95%)
  local copies, waits for them, and re-layouts  7.16 us (3%)
    pallas_call x1, Pallas kernels, window(): pl.pallas_call(kernel, out_shape=(jax.ShapeDtypeStruct((rows, width), BF1...  203 us
    unnamed x8, local copies, waits for them, and re-layouts  6 us

profile of v3, /device:TPU:0, one launch (start us, length us, event | category | flops | bytes accessed | tf_op | source)
XLA Modules:
  0.0 212.6 jit_solution(5235441125078592189)
XLA Ops:
  1.9 1.6 copy.16
  3.5 1.2 copy.17
  4.7 203.5 %window.1 = (bf16[512,2048]{1,0:T(8,128)(2,1)}, bf16[16,256]{1,0:T(8,128)(2,1)}, f32[16,512]{1,0:T(8,128)}) custom-call(bf16[4,128,768]{2,1,0:T(8,128)(2,1)} %bitcast.18, bf16[64,2048]{1,0:T(8,128)(2,1)} %bitcast.21, bf16[512,2048]{1,0:T(8,128)(2,1)} %bitcast.20, bf16[32,256]{1,0:T(8,128)(2,1)} %bitcast.23, bf16[32,512]{1,0:T(8,128)(2,1)} %wd1.1, ...), custom_call_target="tpu_custom_call" | custom-call | tf_op jit(solution)/shard_map/window/pallas_call | solution.py:645
  208.2 0.0 copy-start.1
  208.2 0.0 copy-start
  208.2 3.2 %copy.23 = bf16[1,1,512,2048]{3,2,1,0:T(8,128)(2,1)} copy(bf16[1,1,512,2048]{3,2,1,0:T(8,128)(2,1)} %bitcast.19) | data formatting | bytes 4194304
  211.4 0.0 copy-done.1
  211.4 0.6 copy.24
  212.0 0.0 copy-done
  212.0 0.6 copy.25
Async XLA Ops:
  208.2 3.2 %copy-start.1 = (bf16[16,256]{1,0:T(8,128)(2,1)S(1)}, bf16[16,256]{1,0:T(8,128)(2,1)}, u32[]{:S(2)}) copy-start(bf16[16,256]{1,0:T(8,128)(2,1)} %get-tuple-element.7) | copy-start | bytes 24580
  208.2 3.8 %copy-start = (f32[16,512]{1,0:T(8,128)S(1)}, f32[16,512]{1,0:T(8,128)}, u32[]{:S(2)}) copy-start(f32[16,512]{1,0:T(8,128)} %get-tuple-element.8) | copy-start | bytes 98308

commit v4 on v3

--- a/solution.py
+++ b/solution.py
@@ -210,8 +210,12 @@
         pl.semaphore_signal(barrier, inc=1, device_id=peer, device_id_type=MESH)
     pl.semaphore_wait(barrier, len(peers) + 1)
 
-    def scatter_q(j):
-        return remote(wq.at[lax.rem(x + j, RING)], w_q.at[s, z, y, k], s0q.at[j], r0q.at[x], me.at(dx=j))
+    depth = wq.shape[1]
+    waves = [pl.ds(w * depth // 2, depth // 2) for w in (0, 1)]
+
+    def scatter_q(j, w):
+        return remote(wq.at[lax.rem(x + j, RING), waves[w]], w_q.at[s, z, y, k, waves[w]], s0q.at[w, j],
+                      r0q.at[w, x], me.at(dx=j))
 
     def scatter_o(j):
         cols = pl.ds(pl.multiple_of(lax.rem(x + j, RING) * block, block), block)
@@ -221,9 +225,10 @@
         return remote(wo, w_o1.at[z, y, k], s0w.at[0], r0w.at[k], me.partner())
 
     def start_q():
-        for j in (1, 3, 2):
-            scatter_q(j).start()
-        pltpu.make_async_copy(wq.at[x], w_q.at[s, z, y, k], r0q.at[x]).start()
+        for w in (0, 1):
+            for j in (1, 3, 2):
+                scatter_q(j, w).start()
+            pltpu.make_async_copy(wq.at[x, waves[w]], w_q.at[s, z, y, k, waves[w]], r0q.at[w, x]).start()
 
     def start_o():
         for j in (1, 3, 2):
@@ -289,9 +294,9 @@
             what, peer = xs.at[1 - k, own, high], side
         return remote(what, what, sx.at[n], rx.at[n], peer)
 
-    group = [Spread(me, ref, s1.at[i], r1.at[i], s2.at[i], r2.at[i])
-             for i, ref in enumerate((w_q.at[0], w_o0, w_q.at[1], w_o1))]
-    q0, o0, q1, o1 = group
+    refs = [w_q.at[0, :, :, :, waves[0]], w_q.at[0, :, :, :, waves[1]], w_o0, w_q.at[1], w_o1]
+    q0a, q0b, o0, q1, o1 = [Spread(me, ref, s1.at[i], r1.at[i], s2.at[i], r2.at[i])
+                            for i, ref in enumerate(refs)]
 
     def landed(ref, sem):
         pltpu.make_async_copy(ref, ref, sem).wait()
@@ -307,17 +312,20 @@
         ok = (same > 0.5) & ((j <= i) | (in_i & in_j))
         bias[m] = jnp.where(ok, 0.0, -1e30)
 
-    for kk in (0, 1):
-        landed(w_q.at[0, z, y, kk], r0q.at[kk])
-    q0.own1()
+    for w, spread in enumerate((q0a, q0b)):
+        for kk in (0, 1):
+            landed(w_q.at[0, z, y, kk, waves[w]], r0q.at[w, kk])
+        spread.own1()
     for n in (0, 1, 2):
         x0_copy(n).start()
     section_zero(start_o)
-    q0.pass1()
+    q0a.pass1()
+    q0b.pass1()
+    q0a.own2()
+    q0b.own2()
     m_cp.wait_recv()
     g_cp.wait_recv()
     mask_of(0)
-    q0.own2()
     mask_of(1)
     x0_copy(0).wait_recv()
     x0_copy(5).start()
@@ -329,7 +337,8 @@
         start_q()
         start_w()
 
-    q0.pass2()
+    q0a.pass2()
+    q0b.pass2()
     for kk in (0, 1):
         landed(w_o0.at[z, y, kk], r0o.at[kk])
     o0.own1()
@@ -367,27 +376,27 @@
         scale = lax.rsqrt(ssq[m] * (1.0 / (2 * RING * block)) + EPSILON)
         qkv[m] = (acc[m] * scale).astype(BF16)
 
-    def project1(m):
-        ssq[m] = jnp.zeros_like(ssq[m])
+    halves = [pl.ds(r * rows // 2, rows // 2) for r in (0, 1)]
+
+    def project1(m, r):
+        at = halves[r]
+        squares, total = 0.0, 0.0
         for b in range(0, 2 * RING, 2):
             pieces = []
             for n in (b, b + 1):
-                values = xs[m, n].astype(F32)
-                ssq[m] += jnp.sum(values * values, axis=1, keepdims=True)
+                values = xs[m, n, at].astype(F32)
+                squares += jnp.sum(values * values, axis=1, keepdims=True)
                 pieces.append((values * gains[1, n]).astype(BF16))
-            total = dot(jnp.concatenate(pieces, axis=1), w_q[1, b // 2].reshape(2 * block, acc.shape[2]))
-            if b == 0:
-                acc[m] = total
-            else:
-                acc[m] += total
-        scaled(m)
+            total += dot(jnp.concatenate(pieces, axis=1), w_q[1, b // 2].reshape(2 * block, acc.shape[2]))
+        scale = lax.rsqrt(squares * (1.0 / (2 * RING * block)) + EPSILON)
+        qkv[m, at] = (total * scale).astype(BF16)
 
     hdim = 128
     per = heads.shape[3] // hdim
     q_rows = 128
 
-    def attend(layer, m):
-        for i in range(rows // q_rows):
+    def attend(m, r):
+        for i in range(r * rows // (2 * q_rows), (r + 1) * rows // (2 * q_rows)):
             at = pl.ds(i * q_rows, q_rows)
             for h in range(per):
                 base = 3 * h * hdim
@@ -400,50 +409,44 @@
                 probs = (probs * (1.0 / jnp.sum(probs, axis=1, keepdims=True))).astype(BF16)
                 heads[m, mine, at, h * hdim:(h + 1) * hdim] = dot(probs, vals).astype(BF16)
 
-    h_ring = [[Ring(me, heads.at[m], ring_s.at[layer, m], ring_r.at[layer, m]) for m in (0, 1)]
-              for layer in (0, 1)]
-    x_ring = [Ring(me, xs.at[m], ring_s.at[2, m], ring_r.at[2, m]) for m in (0, 1)]
-
-    def mix0(m):
-        together = jnp.concatenate([heads[m, b] for b in range(2 * RING)], axis=1)
+    units = [(m, r) for m in (0, 1) for r in (0, 1)]
+    h0, h1 = [[Ring(me, heads.at[m, :, halves[r]], ring_s.at[n, m, r], ring_r.at[n, m, r]) for m, r in units]
+              for n in (0, 1)]
+    xr = [Ring(me, xs.at[m, :, halves[r]], ring_s.at[2, m, r], ring_r.at[2, m, r]) for m, r in units]
+
+    def mix0(m, r):
+        at = halves[r]
+        together = jnp.concatenate([heads[m, b, at] for b in range(2 * RING)], axis=1)
         added = dot(together, w_o0[...].reshape(2 * RING * per * hdim, block))
-        xs[m, mine] = (xs[m, mine].astype(F32) + added).astype(BF16)
-
+        xs[m, mine, at] = (xs[m, mine, at].astype(F32) + added).astype(BF16)
+
+    def mixed(u):
+        h0[u].finish()
+        mix0(*units[u])
+        h0[u].drain()
+        xr[u].start()
+
+    def attended(ring, u):
+        attend(*units[u])
+        ring[u].start()
+
+    o0.pass1()
+    for kk in (0, 1):
+        landed(w_q.at[1, z, y, kk, waves[0]], r0q.at[0, 2 + kk])
+        landed(w_q.at[1, z, y, kk, waves[1]], r0q.at[1, 2 + kk])
+    q1.own1()
     for step in (0, 1, 3):
         for m in (0, 1):
             band(m, step, step == 0)
     for n in (0, 1, 2, 5, 6):
         x0_copy(n).wait_send()
-    q0.done()
-    o0.pass1()
+    q0a.done()
+    q0b.done()
+    o0.own2()
     band(0, 2)
     scaled(0)
-    attend(0, 0)
-    h_ring[0][0].start()
-    o0.own2()
-    band(1, 2)
-    scaled(1)
-    attend(0, 1)
-    h_ring[0][1].start()
-    o0.pass2()
-    for kk in (0, 1):
-        landed(w_q.at[1, z, y, kk], r0q.at[2 + kk])
-    q1.own1()
-    h_ring[0][0].direct()
-    h_ring[0][0].far()
-    h_ring[0][0].finish()
-    o0.done()
-    mix0(0)
-    h_ring[0][0].drain()
-    x_ring[0].start()
+    attended(h0, 0)
     q1.pass1()
-    h_ring[0][1].direct()
-    h_ring[0][1].far()
-    h_ring[0][1].finish()
-    mix0(1)
-    h_ring[0][1].drain()
-    x_ring[1].start()
-    q1.own2()
 
     @section_one
     def _():
@@ -451,35 +454,83 @@
             landed(w_o1.at[z, y, kk], r0w.at[kk])
         o1.own1()
 
-    x_ring[0].direct()
-    x_ring[0].far()
+    attended(h0, 1)
+    q1.own2()
+    band(1, 2)
+    scaled(1)
+    h0[0].direct()
+    attended(h0, 2)
+    o0.pass2()
     section_one(o1.pass1)
+    h0[0].far()
+    h0[1].direct()
+    attended(h0, 3)
+    o0.done()
+    mixed(0)
+    h0[1].far()
+    h0[2].direct()
+    mixed(1)
+    h0[2].far()
+    h0[3].direct()
     q1.pass2()
     section_one(o1.own2)
-    x_ring[0].finish()
-    x_ring[1].direct()
+    mixed(2)
+    xr[0].direct()
+    h0[3].far()
+    mixed(3)
+    xr[0].far()
+    xr[1].direct()
+    xr[0].finish()
     q1.done()
-    project1(0)
-    attend(1, 0)
-    h_ring[1][0].start()
-    x_ring[1].far()
+    project1(0, 0)
+    xr[1].far()
+    xr[2].direct()
+    xr[1].finish()
+    project1(0, 1)
     section_one(o1.pass2)
-    x_ring[1].finish()
-    project1(1)
-    h_ring[1][0].direct()
-    attend(1, 1)
-    h_ring[1][1].start()
+    attended(h1, 0)
+    xr[2].far()
+    xr[3].direct()
+    attended(h1, 1)
+    xr[2].finish()
+    project1(1, 0)
+    xr[3].far()
+    h1[0].direct()
+    xr[3].finish()
+    project1(1, 1)
+    h1[0].far()
+    h1[1].direct()
+    attended(h1, 2)
+    h1[1].far()
+    attended(h1, 3)
 
     @section_zero
     def _():
         for j in range(RING):
             hid[:, j * block:(j + 1) * block] = xs[k, c * RING + j]
 
-    h_ring[1][0].far()
-    h_ring[1][1].direct()
-    h_ring[1][1].far()
-    h_ring[1][0].finish()
-    h_ring[1][1].finish()
+    h1[2].direct()
+    h1[2].far()
+    h1[3].direct()
+
+    def mix1(r):
+        at = halves[r]
+        together = jnp.concatenate([heads[k, b, at] for b in range(2 * RING)], axis=1)
+        for j in range(RING):
+            cols = slice(j * block, (j + 1) * block)
+            added = dot(together, w_o1[:, :, :, :, cols].reshape(2 * RING * per * hdim, block))
+            hid[at, cols] = (xs[k, c * RING + j, at].astype(F32) + added).astype(BF16)
+
+    for u in (0, 1, 2):
+        h1[u].finish()
+
+    @section_one
+    def _():
+        o1.done()
+        mix1(0)
+
+    h1[3].far()
+    h1[3].finish()
 
     def tail_copy(n):
         if n == 0:
@@ -513,12 +564,7 @@
             give(7).wait_recv()
             give(8).wait_recv()
 
-        o1.done()
-        together = jnp.concatenate([heads[k, b] for b in range(2 * RING)], axis=1)
-        for j in range(RING):
-            at = slice(j * block, (j + 1) * block)
-            added = dot(together, w_o1[:, :, :, :, at].reshape(2 * RING * per * hdim, block))
-            hid[:, at] = (xs[k, c * RING + j].astype(F32) + added).astype(BF16)
+        mix1(1)
         ri = lax.broadcasted_iota(jnp.int32, (img_tok, rows), 0)
         ci = lax.broadcasted_iota(jnp.int32, (img_tok, rows), 1)
         take = (ci == ri + metas[k, 1:2, :]).astype(F32).astype(BF16)
@@ -554,7 +600,8 @@
         tail_copy(0).wait_send()
 
     for j in (1, 2, 3):
-        scatter_q(j).wait_send()
+        for w in (0, 1):
+            scatter_q(j, w).wait_send()
 
     @section_zero
     def _():
@@ -573,9 +620,9 @@
 
     g_cp.wait_send()
     m_cp.wait_send()
-    for g in (q0, o0, q1):
+    for g in (q0a, q0b, o0, q1):
         g.drain()
-    for r in h_ring[1] + x_ring:
+    for r in h1 + xr:
         r.drain()
 
     @pl.when((s == 1) & (c == 1))
@@ -637,9 +684,9 @@
         vm((2, pix, channels), F32),
         vm((RING, pix, channels), F32),
         vm((RING, pix, channels), F32),
-        dma((4,)), dma((4,)), dma((4,)), dma((2,)), dma((1,)), dma((2,)),
-        dma((4, 2, 4)), dma((4, 2, 4)), dma((4, 2, 4)), dma((4, 2, 4)),
-        dma((3, 2, 8)), dma((3, 2, 8)), dma((9,)), dma((9,)), dma((13,)), dma((11,)), dma((4,)),
+        dma((2, 4)), dma((2, 4)), dma((4,)), dma((2,)), dma((1,)), dma((2,)),
+        dma((5, 2, 4)), dma((5, 2, 4)), dma((5, 2, 4)), dma((5, 2, 4)),
+        dma((3, 2, 2, 8)), dma((3, 2, 2, 8)), dma((9,)), dma((9,)), dma((13,)), dma((11,)), dma((4,)),
     ]
     sm = pl.BlockSpec(memory_space=pltpu.SMEM)
     return pl.pallas_call(

time: 214 us -> 199 us (0.930)
  Pallas kernels: 203 us -> 188 us
    pallas_call x1, Pallas kernels: 203 us -> 188 us  [window(): pl.pallas_call(kernel, out_shape=(jax.ShapeDtypeStruct((rows, width), BF1...]
where the time goes in v4:
time: 199 us; the launch traced here: 197 us
  Pallas kernels  188 us (94%)
  local copies, waits for them, and re-layouts  7.16 us (4%)
    pallas_call x1, Pallas kernels, window(): pl.pallas_call(kernel, out_shape=(jax.ShapeDtypeStruct((rows, width), BF1...  188 us
    unnamed x8, local copies, waits for them, and re-layouts  6 us

profile of v4, /device:TPU:0, one launch (start us, length us, event | category | flops | bytes accessed | tf_op | source)
XLA Modules:
  0.0 197.3 jit_solution(16735350923318869203)
XLA Ops:
  1.9 1.6 copy.16
  3.5 1.2 copy.17
  4.7 188.2 %window.1 = (bf16[512,2048]{1,0:T(8,128)(2,1)}, bf16[16,256]{1,0:T(8,128)(2,1)}, f32[16,512]{1,0:T(8,128)}) custom-call(bf16[4,128,768]{2,1,0:T(8,128)(2,1)} %bitcast.18, bf16[64,2048]{1,0:T(8,128)(2,1)} %bitcast.21, bf16[512,2048]{1,0:T(8,128)(2,1)} %bitcast.20, bf16[32,256]{1,0:T(8,128)(2,1)} %bitcast.23, bf16[32,512]{1,0:T(8,128)(2,1)} %wd1.1, ...), custom_call_target="tpu_custom_call" | custom-call | tf_op jit(solution)/shard_map/window/pallas_call | solution.py:692
  192.9 0.0 copy-start.1
  192.9 0.0 copy-start
  192.9 3.2 %copy.23 = bf16[1,1,512,2048]{3,2,1,0:T(8,128)(2,1)} copy(bf16[1,1,512,2048]{3,2,1,0:T(8,128)(2,1)} %bitcast.19) | data formatting | bytes 4194304
  196.1 0.0 copy-done.1
  196.1 0.6 copy.24
  196.7 0.0 copy-done
  196.7 0.6 copy.25
Async XLA Ops:
  192.9 3.2 %copy-start.1 = (bf16[16,256]{1,0:T(8,128)(2,1)S(1)}, bf16[16,256]{1,0:T(8,128)(2,1)}, u32[]{:S(2)}) copy-start(bf16[16,256]{1,0:T(8,128)(2,1)} %get-tuple-element.7) | copy-start | bytes 24580
  192.9 3.8 %copy-start = (f32[16,512]{1,0:T(8,128)S(1)}, f32[16,512]{1,0:T(8,128)}, u32[]{:S(2)}) copy-start(f32[16,512]{1,0:T(8,128)} %get-tuple-element.8) | copy-start | bytes 98308

commit v5 on v4

--- a/solution.py
+++ b/solution.py
@@ -178,7 +178,7 @@
     wq, wo, tokens, patches_t, wd1, wd2, wu1, wu2_t, gain, segment, start_in, count_in, cot_t,
     hid, pred, grad,
     w_q, w_o0, w_o1, xs, heads, acc, qkv, bias, ssq, gains, metas, skip, down2, up1,
-    part, got, upper, cots, ups, p_own, p_in, g_own, g_in, pair, ys, zs,
+    part, got, upper, cots, ups, p_own, p_in, g_own, g_in, ys, zs,
     s0q, r0q, s0o, r0o, s0w, r0w, s1, r1, s2, r2, ring_s, ring_r, sx, rx, st, rt, loc,
 ):
     me = Place()
@@ -202,7 +202,12 @@
     metas[k, 2:3, :] = jnp.full((1, rows), count_in[0], jnp.int32)
     metas[k, 3:8, :] = jnp.zeros((5, rows), jnp.int32)
 
-    peers = ([me.at(dx=j) for j in (1, 2, 3)] + [me.at(dy=j) for j in (1, 2, 3)]
+    place = 2 * y + k
+
+    def plane(n):
+        return {"section": s, "tp": c, "dp": 8 * z + lax.rem(place + n, 8)}
+
+    peers = ([me.at(dx=j) for j in (1, 2, 3)] + [plane(n) for n in range(1, 8)]
              + [me.at(dz=j) for j in (1, 2, 3)] + [side])
     across = dict(me.at(dx=2), tp=1 - c)
     barrier = pltpu.get_barrier_semaphore()
@@ -241,7 +246,7 @@
         pltpu.make_async_copy(wo, w_o1.at[z, y, k], r0w.at[k]).start()
 
     section_zero, section_one = pl.when(s == 0), pl.when(s == 1)
-    section_zero(start_q)
+    start_q()
 
     for cp in loads:
         cp.wait()
@@ -319,6 +324,7 @@
     for n in (0, 1, 2):
         x0_copy(n).start()
     section_zero(start_o)
+    section_one(start_w)
     q0a.pass1()
     q0b.pass1()
     q0a.own2()
@@ -331,11 +337,6 @@
     x0_copy(5).start()
     x0_copy(1).wait_recv()
     x0_copy(6).start()
-
-    @section_one
-    def _():
-        start_q()
-        start_w()
 
     q0a.pass2()
     q0b.pass2()
@@ -431,10 +432,6 @@
         ring[u].start()
 
     o0.pass1()
-    for kk in (0, 1):
-        landed(w_q.at[1, z, y, kk, waves[0]], r0q.at[0, 2 + kk])
-        landed(w_q.at[1, z, y, kk, waves[1]], r0q.at[1, 2 + kk])
-    q1.own1()
     for step in (0, 1, 3):
         for m in (0, 1):
             band(m, step, step == 0)
@@ -443,10 +440,14 @@
     q0a.done()
     q0b.done()
     o0.own2()
+    for kk in (0, 1):
+        landed(w_q.at[1, z, y, kk, waves[0]], r0q.at[0, 2 + kk])
+        landed(w_q.at[1, z, y, kk, waves[1]], r0q.at[1, 2 + kk])
+    q1.own1()
     band(0, 2)
     scaled(0)
     attended(h0, 0)
-    q1.pass1()
+    attended(h0, 1)
 
     @section_one
     def _():
@@ -454,17 +455,17 @@
             landed(w_o1.at[z, y, kk], r0w.at[kk])
         o1.own1()
 
-    attended(h0, 1)
-    q1.own2()
     band(1, 2)
     scaled(1)
     h0[0].direct()
     attended(h0, 2)
+    q1.pass1()
     o0.pass2()
-    section_one(o1.pass1)
     h0[0].far()
     h0[1].direct()
     attended(h0, 3)
+    q1.own2()
+    section_one(o1.pass1)
     o0.done()
     mixed(0)
     h0[1].far()
@@ -472,12 +473,12 @@
     mixed(1)
     h0[2].far()
     h0[3].direct()
-    q1.pass2()
-    section_one(o1.own2)
     mixed(2)
     xr[0].direct()
     h0[3].far()
     mixed(3)
+    q1.pass2()
+    section_one(o1.own2)
     xr[0].far()
     xr[1].direct()
     xr[0].finish()
@@ -487,11 +488,11 @@
     xr[2].direct()
     xr[1].finish()
     project1(0, 1)
-    section_one(o1.pass2)
     attended(h1, 0)
     xr[2].far()
     xr[3].direct()
     attended(h1, 1)
+    section_one(o1.pass2)
     xr[2].finish()
     project1(1, 0)
     xr[3].far()
@@ -535,17 +536,15 @@
     def tail_copy(n):
         if n == 0:
             return remote(part, got, st.at[0], rt.at[0], side)
-        if n == 2:
-            return remote(pair.at[0], pair.at[1], st.at[2], rt.at[2], me.partner())
-        if n < 6:
-            return remote(ys.at[y], ys.at[y], st.at[n], rt.at[n], me.at(dy=n - 2))
-        return remote(zs.at[z], zs.at[z], st.at[n], rt.at[n], me.at(dz=n - 5))
+        if n < 8:
+            return remote(ys.at[place], ys.at[place], st.at[n], rt.at[n], plane(n))
+        return remote(zs.at[z], zs.at[z], st.at[n], rt.at[n], me.at(dz=n - 7))
 
     def result_copy(n, core):
         src, dst = ((p_own, p_in), (g_own, g_in))[n]
         peer = side if core is None else dict(me.at(dx=2), tp=core)
         index = 0 if core is None else core
-        return remote(src, dst, st.at[9 + 2 * n + index], rt.at[9 + n], peer)
+        return remote(src, dst, st.at[11 + 2 * n + index], rt.at[11 + n], peer)
 
     def send_result(n):
         @pl.when(c == 0)
@@ -568,32 +567,32 @@
         ri = lax.broadcasted_iota(jnp.int32, (img_tok, rows), 0)
         ci = lax.broadcasted_iota(jnp.int32, (img_tok, rows), 1)
         take = (ci == ri + metas[k, 1:2, :]).astype(F32).astype(BF16)
-        total = jnp.zeros(part.shape, F32)
+        total = jnp.zeros(got.shape, F32)
         for j in range(RING):
             at = slice(j * block, (j + 1) * block)
             total = total + dot(dot(take, hid[:, at]).astype(BF16), up1[at, :])
-        part[...] = total
+        part[...] = total.astype(BF16)
         tail_copy(0).start()
         tail_copy(0).wait_recv()
-        value = part[...] + got[...] + skip[...].astype(F32)
+        value = total + got[...].astype(F32) + skip[...].astype(F32)
         upper[...] = (value / (1.0 + jnp.exp(-value))).astype(BF16)
         present = metas[k, 2:3, :img_tok] > 0
         weighted = jnp.where(present, cots[...].astype(F32), 0.0).astype(BF16)
-        pair[0] = dot(weighted, upper[...])
-        tail_copy(2).start()
+        ys[place] = dot(weighted, upper[...])
+        for n in range(1, 8):
+            tail_copy(n).start()
         guess = lax.dot_general(ups[...], upper[...], (((1,), (1,)), ((), ())), preferred_element_type=F32)
         p_own[...] = jnp.where(present, guess, 0.0).astype(BF16)
         send_result(0)
-        tail_copy(2).wait()
-        ys[y] = pair[0] + pair[1]
-        for n in (3, 4, 5):
+        for n in range(1, 8):
+            tail_copy(n).wait()
+        in_plane = ys[0]
+        for n in range(1, 8):
+            in_plane = in_plane + ys[n]
+        zs[z] = in_plane
+        for n in (8, 9, 10):
             tail_copy(n).start()
-        for n in (3, 4, 5):
-            tail_copy(n).wait()
-        zs[z] = ys[0] + ys[1] + ys[2] + ys[3]
-        for n in (6, 7, 8):
-            tail_copy(n).start()
-        for n in (6, 7, 8):
+        for n in (8, 9, 10):
             tail_copy(n).wait()
         g_own[...] = zs[0] + zs[1] + zs[2] + zs[3]
         send_result(1)
@@ -672,8 +671,8 @@
         vm((img_tok, channels), BF16),
         vm(wd2.shape, BF16),
         vm(wu1.shape, BF16),
-        vm((img_tok, channels), F32),
-        vm((img_tok, channels), F32),
+        vm((img_tok, channels), BF16),
+        vm((img_tok, channels), BF16),
         vm((img_tok, channels), BF16),
         vm(cot_t.shape, BF16),
         vm(wu2_t.shape, BF16),
@@ -681,12 +680,11 @@
         vm((pix, img_tok), BF16),
         vm((pix, channels), F32),
         vm((pix, channels), F32),
-        vm((2, pix, channels), F32),
-        vm((RING, pix, channels), F32),
+        vm((2 * RING, pix, channels), F32),
         vm((RING, pix, channels), F32),
         dma((2, 4)), dma((2, 4)), dma((4,)), dma((2,)), dma((1,)), dma((2,)),
         dma((5, 2, 4)), dma((5, 2, 4)), dma((5, 2, 4)), dma((5, 2, 4)),
-        dma((3, 2, 2, 8)), dma((3, 2, 2, 8)), dma((9,)), dma((9,)), dma((13,)), dma((11,)), dma((4,)),
+        dma((3, 2, 2, 8)), dma((3, 2, 2, 8)), dma((9,)), dma((9,)), dma((15,)), dma((13,)), dma((4,)),
     ]
     sm = pl.BlockSpec(memory_space=pltpu.SMEM)
     return pl.pallas_call(

time: 199 us -> 192 us (0.965)
  Pallas kernels: 188 us -> 182 us
    pallas_call x1, Pallas kernels: 188 us -> 182 us  [window(): pl.pallas_call(kernel, out_shape=(jax.ShapeDtypeStruct((rows, width), BF1...]
where the time goes in v5:
time: 192 us; the launch traced here: 191 us
  Pallas kernels  182 us (95%)
  local copies, waits for them, and re-layouts  7.16 us (4%)
  between operations  1.96 us (1%)
    pallas_call x1, Pallas kernels, window(): pl.pallas_call(kernel, out_shape=(jax.ShapeDtypeStruct((rows, width), BF1...  182 us
    unnamed x8, local copies, waits for them, and re-layouts  6 us

profile of v5, /device:TPU:0, one launch (start us, length us, event | category | flops | bytes accessed | tf_op | source)
XLA Modules:
  0.0 190.8 jit_solution(14025689465683436051)
XLA Ops:
  1.9 1.6 copy.16
  3.5 1.2 copy.17
  4.7 181.7 %window.1 = (bf16[512,2048]{1,0:T(8,128)(2,1)}, bf16[16,256]{1,0:T(8,128)(2,1)}, f32[16,512]{1,0:T(8,128)}) custom-call(bf16[4,128,768]{2,1,0:T(8,128)(2,1)} %bitcast.18, bf16[64,2048]{1,0:T(8,128)(2,1)} %bitcast.21, bf16[512,2048]{1,0:T(8,128)(2,1)} %bitcast.20, bf16[32,256]{1,0:T(8,128)(2,1)} %bitcast.23, bf16[32,512]{1,0:T(8,128)(2,1)} %wd1.1, ...), custom_call_target="tpu_custom_call" | custom-call | tf_op jit(solution)/shard_map/window/pallas_call | solution.py:690
  186.4 0.0 copy-start.1
  186.4 0.0 copy-start
  186.4 3.2 %copy.23 = bf16[1,1,512,2048]{3,2,1,0:T(8,128)(2,1)} copy(bf16[1,1,512,2048]{3,2,1,0:T(8,128)(2,1)} %bitcast.19) | data formatting | bytes 4194304
  189.6 0.0 copy-done.1
  189.6 0.6 copy.24
  190.2 0.0 copy-done
  190.2 0.6 copy.25
Async XLA Ops:
  186.4 3.2 %copy-start.1 = (bf16[16,256]{1,0:T(8,128)(2,1)S(1)}, bf16[16,256]{1,0:T(8,128)(2,1)}, u32[]{:S(2)}) copy-start(bf16[16,256]{1,0:T(8,128)(2,1)} %get-tuple-element.7) | copy-start | bytes 24580
  186.4 3.8 %copy-start = (f32[16,512]{1,0:T(8,128)S(1)}, f32[16,512]{1,0:T(8,128)}, u32[]{:S(2)}) copy-start(f32[16,512]{1,0:T(8,128)} %get-tuple-element.8) | copy-start | bytes 98308

commit v6 on v5

--- a/solution.py
+++ b/solution.py
@@ -478,11 +478,11 @@
     h0[3].far()
     mixed(3)
     q1.pass2()
-    section_one(o1.own2)
     xr[0].far()
     xr[1].direct()
     xr[0].finish()
     q1.done()
+    section_one(o1.own2)
     project1(0, 0)
     xr[1].far()
     xr[2].direct()
@@ -492,9 +492,9 @@
     xr[2].far()
     xr[3].direct()
     attended(h1, 1)
-    section_one(o1.pass2)
     xr[2].finish()
     project1(1, 0)
+    section_one(o1.pass2)
     xr[3].far()
     h1[0].direct()
     xr[3].finish()
@@ -505,11 +505,6 @@
     h1[1].far()
     attended(h1, 3)
 
-    @section_zero
-    def _():
-        for j in range(RING):
-            hid[:, j * block:(j + 1) * block] = xs[k, c * RING + j]
-
     h1[2].direct()
     h1[2].far()
     h1[3].direct()
@@ -532,6 +527,11 @@
 
     h1[3].far()
     h1[3].finish()
+
+    @section_zero
+    def _():
+        for j in range(RING):
+            hid[:, j * block:(j + 1) * block] = xs[k, c * RING + j]
 
     def tail_copy(n):
         if n == 0:

time: 192 us -> 192 us (level)
  no operation moved by 1% of the time
where the time goes in v6:
time: 192 us; the launch traced here: 190 us
  Pallas kernels  181 us (94%)
  local copies, waits for them, and re-layouts  7.16 us (4%)
  between operations  1.96 us (1%)
    pallas_call x1, Pallas kernels, window(): pl.pallas_call(kernel, out_shape=(jax.ShapeDtypeStruct((rows, width), BF1...  181 us
    unnamed x8, local copies, waits for them, and re-layouts  6 us

profile of v6, /device:TPU:0, one launch (start us, length us, event | category | flops | bytes accessed | tf_op | source)
XLA Modules:
  0.0 190.5 jit_solution(9740927972676790353)
XLA Ops:
  1.9 1.6 copy.16
  3.5 1.2 copy.17
  4.7 181.4 %window.1 = (bf16[512,2048]{1,0:T(8,128)(2,1)}, bf16[16,256]{1,0:T(8,128)(2,1)}, f32[16,512]{1,0:T(8,128)}) custom-call(bf16[4,128,768]{2,1,0:T(8,128)(2,1)} %bitcast.18, bf16[64,2048]{1,0:T(8,128)(2,1)} %bitcast.21, bf16[512,2048]{1,0:T(8,128)(2,1)} %bitcast.20, bf16[32,256]{1,0:T(8,128)(2,1)} %bitcast.23, bf16[32,512]{1,0:T(8,128)(2,1)} %wd1.1, ...), custom_call_target="tpu_custom_call" | custom-call | tf_op jit(solution)/shard_map/window/pallas_call | solution.py:690
  186.1 0.0 copy-start.1
  186.1 0.0 copy-start
  186.1 3.2 %copy.23 = bf16[1,1,512,2048]{3,2,1,0:T(8,128)(2,1)} copy(bf16[1,1,512,2048]{3,2,1,0:T(8,128)(2,1)} %bitcast.19) | data formatting | bytes 4194304
  189.3 0.0 copy-done.1
  189.3 0.6 copy.24
  189.9 0.0 copy-done
  189.9 0.6 copy.25
Async XLA Ops:
  186.1 3.2 %copy-start.1 = (bf16[16,256]{1,0:T(8,128)(2,1)S(1)}, bf16[16,256]{1,0:T(8,128)(2,1)}, u32[]{:S(2)}) copy-start(bf16[16,256]{1,0:T(8,128)(2,1)} %get-tuple-element.7) | copy-start | bytes 24580
  186.1 3.8 %copy-start = (f32[16,512]{1,0:T(8,128)S(1)}, f32[16,512]{1,0:T(8,128)}, u32[]{:S(2)}) copy-start(f32[16,512]{1,0:T(8,128)} %get-tuple-element.8) | copy-start | bytes 98308
